TPU v7x, 256 devices: a whole 4x4x8 slice. The times are simulated.
256 devices in a mesh: img: 32 (over y, z), grp: 8 (over x, core).
Axes of the slice: x: 4, y: 4, z: 8, core: 2. Of those that a mesh axis runs over, the one named last changes fastest.
Arguments:
- images: bfloat16 [8192, 128, 512], P(('img', 'grp')), may hold values from -18 to 18
- group_ids: int32 [8192], P(('img', 'grp')), may hold values from 0 to 7
- counts: int32 [128], replicated, may hold values from 1 to 128, as said below
- radial_basis: bfloat16 [128, 128, 128], replicated, may hold values from -0.5 to 0.5
- ctf_gain: float32 [8, 128], replicated, may hold values from 0.2 to 2
- noise_var: float32 [128], replicated, may hold values from 0.25 to 2
Outputs:
- denoised: bfloat16 [8192, 128, 512], P(('img', 'grp'))
Inputs may be any that keep to these rules, and one draw needn't show every extreme that they name: In every aligned block of 4 frequencies the counts sum to exactly 320 and the largest is exactly 128.
All inputs are finite; a program needn't handle non-finite values.
Results may differ from a plain program's by a relative error of at most 0.0063.
The roundings to bfloat16 on the way count: a program that leaves them out, or rounds other values in their place, can miss the bound.
Values may be sent and summed in bfloat16 or wider, within the bound.
A program may use at most 128 MiB of HBM per device.

v0:
```python
import functools
import math

import jax
import jax.numpy as jnp
from jax import lax
from jax.experimental import pallas as pl
from jax.experimental.pallas import tpu as pltpu
from jax.sharding import PartitionSpec as P

NS_ITERS = 7
SIDE = 4
MESH_ID = pl.DeviceIdType.MESH
VMEM = pl.BlockSpec(memory_space=pltpu.VMEM)
SMEM = pl.BlockSpec(memory_space=pltpu.SMEM)
F32 = jnp.float32
BF16 = jnp.bfloat16


def place():
    img = lax.axis_index("img")
    grp = lax.axis_index("grp")
    return grp // 2, img // 8, img % 8, grp % 2


def owner_index(x, y, z):
    return x * 8 + y * 2 + z % 2


def hops(step):
    return min(step, SIDE - step)


def exchange_steps():
    steps = [(a, b, c) for a in range(SIDE) for b in range(SIDE) for c in range(2)]
    steps.remove((0, 0, 0))
    steps.sort(key=lambda s: -(hops(s[0]) + hops(s[1]) + s[2]))
    return steps


def exchange_kernel(with_ids, *refs):
    if with_ids:
        data, ids, out, ids_out, local, send, recv, local_ids, send_ids, recv_ids = refs
    else:
        data, out, local, send, recv = refs
    x, y, z, core = place()
    me = owner_index(x, y, z)
    steps = exchange_steps()
    peers = []
    for a, b, c in steps:
        px, py, pz = (x + a) % SIDE, (y + b) % SIDE, z // 2 * 2 + (z + c) % 2
        peers.append(({"img": py * 8 + pz, "grp": px * 2 + core}, owner_index(px, py, pz)))
    barrier = pltpu.get_barrier_semaphore()
    for device, _ in peers:
        pl.semaphore_signal(barrier, inc=1, device_id=device, device_id_type=MESH_ID)
    own = [pltpu.make_async_copy(data.at[me], out.at[me], local)]
    if with_ids:
        own.append(pltpu.make_async_copy(ids, ids_out.at[me], local_ids))
    for copy in own:
        copy.start()
    pl.semaphore_wait(barrier, len(peers))
    copies = []
    for i, (device, index) in enumerate(peers):
        copies.append(
            pltpu.make_async_remote_copy(
                data.at[index], out.at[me], send.at[i], recv.at[i],
                device_id=device, device_id_type=MESH_ID,
            )
        )
        if with_ids:
            copies.append(
                pltpu.make_async_remote_copy(
                    ids, ids_out.at[me], send_ids.at[i], recv_ids.at[i],
                    device_id=device, device_id_type=MESH_ID,
                )
            )
    for copy in copies:
        copy.start()
    for copy in own + copies:
        copy.wait()


def exchange(data, ids, collective_id):
    count = data.shape[0] - 1
    dma = pltpu.SemaphoreType.DMA
    scratch = [dma, dma((count,)), dma((count,))]
    operands, shapes = [data], [jax.ShapeDtypeStruct(data.shape, data.dtype)]
    if ids is not None:
        operands.append(ids)
        shapes.append(jax.ShapeDtypeStruct((data.shape[0], *ids.shape), ids.dtype))
        scratch = scratch * 2
    return pl.pallas_call(
        functools.partial(exchange_kernel, ids is not None),
        out_shape=shapes,
        in_specs=[VMEM] * len(operands),
        out_specs=[VMEM] * len(operands),
        scratch_shapes=scratch,
        compiler_params=pltpu.CompilerParams(collective_id=collective_id, has_side_effects=True),
        name="exchange",
    )(*operands)


def lanes(shape):
    return lax.broadcasted_iota(jnp.int32, shape, len(shape) - 1)


def tile(index):
    return pl.ds(pl.multiple_of(index * 128, 128), 128)


def block_slots(counts, first):
    offsets, offset = [], 0
    for j in range(4):
        count = counts[first + j]
        offsets.append((offset, count))
        offset = offset + count
    return offsets


def pack_kernel(counts, coeffs, out, wide):
    lane = lanes((64, 128))

    @pl.loop(0, 32)
    def _(block):
        wide[...] = jnp.zeros_like(wide)
        for j, (offset, count) in enumerate(block_slots(counts, block * 4)):
            value = jnp.where(lane < count, coeffs[block * 4 + j].astype(F32), 0.0)
            shift, first = offset % 128, offset // 128
            turned = pltpu.roll(value, shift, 1)
            wide[:, tile(first)] += jnp.where(lane >= shift, turned, 0.0)
            wide[:, tile(first + 1)] += jnp.where(lane < shift, turned, 0.0)
        fold_slots(wide[:, 0:128], wide[:, 128:256], wide[:, 256:384], out.at[block])


def fold_slots(low, middle, high, out):
    out[0:64] = low.astype(BF16)
    out[64:128] = middle.astype(BF16)
    lane = lanes((32, 128))
    out[128:160] = jnp.where(lane < 64, high[0:32], pltpu.roll(high[32:64], 64, 1)).astype(BF16)


def unfold_slots(high):
    lane = lanes((32, 128))
    high = high.astype(F32)
    first = jnp.where(lane < 64, high, 0.0)
    second = jnp.where(lane < 64, pltpu.roll(high, 64, 1), 0.0)
    return jnp.concatenate([first, second], 0)


def unpack_kernel(counts, packed, out, wide):
    lane = lanes((64, 128))
    wide[...] = jnp.zeros_like(wide)

    @pl.loop(0, 32)
    def _(block):
        wide[:, 0:128] = packed[block, 0:64].astype(F32)
        wide[:, 128:256] = packed[block, 64:128].astype(F32)
        wide[:, 256:384] = unfold_slots(packed[block, 128:160])
        for j, (offset, count) in enumerate(block_slots(counts, block * 4)):
            shift, first = offset % 128, offset // 128
            back = (128 - shift) % 128
            low = pltpu.roll(wide[:, tile(first)], back, 1)
            high = pltpu.roll(wide[:, tile(first + 1)], back, 1)
            value = jnp.where(lane < 128 - shift, low, high)
            out[block * 4 + j] = jnp.where(lane < count, value, 0.0).astype(BF16)


def chunk_slots(packed, start):
    rows = [packed[start + s] for s in range(4)]
    low = jnp.concatenate([r[0:64] for r in rows], 0).astype(F32)
    middle = jnp.concatenate([r[64:128] for r in rows], 0).astype(F32)
    high = jnp.concatenate([unfold_slots(r[128:160]) for r in rows], 0)
    return low, middle, high


def gram_kernel(counts, gains, packed, ids, out, gram, table, member):
    x, y, z, _ = place()
    first_freq = owner_index(x, y, z) * 4
    slots = block_slots(counts, first_freq)
    gram[...] = jnp.zeros_like(gram)
    row = lax.broadcasted_iota(jnp.int32, (8, 512), 0)
    lane = lanes((8, 512))
    slot_gain = jnp.zeros((8, 512), F32)
    for j, (offset, count) in enumerate(slots):
        column = jnp.zeros((8, 512), F32)
        for g in range(8):
            column = jnp.where(row == g, gains[g, first_freq + j], column)
        here = ((lane >= offset) & (lane < offset + count)) | (lane == 384 + j)
        slot_gain = jnp.where(here, column, slot_gain)
    high = slot_gain.astype(BF16).astype(F32)
    middle = (slot_gain - high).astype(BF16).astype(F32)
    low = slot_gain - high - middle
    table[...] = jnp.concatenate([high, middle, low, jnp.zeros((104, 512), F32)], 0).astype(BF16)
    row = lax.broadcasted_iota(jnp.int32, (384, 128), 0)
    lane = lanes((384, 128))
    inside = jnp.zeros((384, 128), F32)
    for j, (offset, count) in enumerate(slots):
        inside = jnp.where((lane == j) & (row >= offset) & (row < offset + count), 1.0, inside)
    member[...] = inside.astype(BF16)
    lane = lanes((256, 128))
    wanted = jnp.where(lane < 24, lane % 8, -1).astype(F32)

    def chunk(i, sums):
        fourth, total = sums
        value = jnp.concatenate(chunk_slots(packed, i * 4), 1)
        group = ids[pl.ds(pl.multiple_of(i * 256, 256), 256), :].astype(F32)
        onehot = jnp.where(group == wanted, 1.0, 0.0).astype(BF16)
        gain = jnp.dot(onehot, table[...], preferred_element_type=F32)
        scaled = (value * gain[:, 0:384]).astype(BF16)
        sums = lax.dot_general(
            scaled, scaled, (((0,), (0,)), ((), ())), preferred_element_type=F32
        )
        for t in range(3):
            gram[t, 0:384] += sums[:, t * 128 : t * 128 + 128]
        square = value * value
        upper = square.astype(BF16)
        lower = (square - upper.astype(F32)).astype(BF16)
        norms = jnp.dot(upper, member[...], preferred_element_type=F32)
        norms += jnp.dot(lower, member[...], preferred_element_type=F32)
        weight = gain[:, 384:512] * gain[:, 384:512]
        fourth += jnp.sum(weight * norms * norms, 0, keepdims=True)
        total += jnp.sum(weight, 0, keepdims=True)
        return fourth, total

    nothing = jnp.zeros((1, 128), F32)
    fourth, total = lax.fori_loop(0, 8, chunk, (nothing, nothing))
    row = lax.broadcasted_iota(jnp.int32, (128, 128), 0)
    lane = lanes((128, 128))
    for j, (offset, count) in enumerate(slots):
        shift, first = offset % 128, offset // 128
        back = (128 - shift) % 128
        low = pltpu.roll(gram[first, pl.ds(offset, 128)], back, 1)
        high = pltpu.roll(gram[first + 1, pl.ds(offset, 128)], back, 1)
        value = jnp.where(lane < 128 - shift, low, high)
        out[j, 0:128] = jnp.where((lane < count) & (row < count), value, 0.0)
        out[j, 128:136] = jnp.concatenate([fourth, total, jnp.zeros((6, 128), F32)], 0)


def reduce_kernel(part, out, other, mine, send, recv):
    x, y, z, core = place()
    quarter, low = z // 2, z % 2
    partner = {"img": y * 8 + z, "grp": x * 2 + 1 - core}
    column = []
    for step in (2, 1, 3):
        column.append({"img": y * 8 + (quarter + step) % 4 * 2 + low, "grp": x * 2 + core})
    barrier = pltpu.get_barrier_semaphore()
    for device in [partner] + column:
        pl.semaphore_signal(barrier, inc=1, device_id=device, device_id_type=MESH_ID)
    pl.semaphore_wait(barrier, 4)
    swap = pltpu.make_async_remote_copy(
        part.at[pl.ds((1 - core) * 2, 2)], other, send.at[0], recv.at[0],
        device_id=partner, device_id_type=MESH_ID,
    )
    swap.start()
    swap.wait()
    both = part[pl.ds(core * 2, 2)] + other[...]
    mine[...] = both
    copies = []
    for i, device in enumerate(column):
        copies.append(
            pltpu.make_async_remote_copy(
                mine, out.at[quarter], send.at[i + 1], recv.at[i + 1],
                device_id=device, device_id_type=MESH_ID,
            )
        )
    for copy in copies:
        copy.start()
    out[quarter] = both
    for copy in copies:
        copy.wait()


def split(value):
    high = value.astype(BF16)
    return high, (value - high.astype(F32)).astype(BF16)


def right_side(value):
    high, low = split(value)
    return jnp.concatenate(
        [jnp.concatenate([high, low], 1), jnp.concatenate([high, jnp.zeros_like(high)], 1)], 0
    )


def product(left, right):
    high, low = split(left)
    wide = jnp.dot(jnp.concatenate([high, low], 1), right, preferred_element_type=F32)
    return wide[:, 0:128] + wide[:, 128:256]


def total_of(value):
    return jnp.sum(jnp.sum(value, 0, keepdims=True), 1, keepdims=True)


def filter_kernel(images, counts, gains, noise, parts, out, cov_ref, cov_right, size, trace):
    x, y, z, core = place()
    first_freq = owner_index(x, y, z) * 4 + core * 2
    row = lax.broadcasted_iota(jnp.int32, (128, 128), 0)
    lane = lanes((128, 128))
    line = lanes((1, 128))
    for j in range(2):
        block = ((parts[0, j] + parts[1, j]) + parts[2, j]) + parts[3, j]
        count = counts[first_freq + j]
        here = line == core * 2 + j
        fourth = jnp.sum(jnp.where(here, block[128:129], 0.0), 1, keepdims=True)
        total = jnp.sum(jnp.where(here, block[129:130], 0.0), 1, keepdims=True)
        sample = block[0:128] / total
        ident = jnp.where((row == lane) & (row < count), 1.0, 0.0)
        level = total_of(sample * ident) / count.astype(F32)
        off_level = sample - level * ident
        spread = total_of(off_level * off_level)
        excess = (fourth / total - total_of(sample * sample)) / (2.0 * images)
        weight = excess / (excess + spread)
        cov = (1.0 - weight) * sample + (weight * level) * ident
        cov_ref[j] = cov
        cov_right[j] = right_side(cov)
        size[j] = jnp.broadcast_to(total_of(cov * cov), (8, 128))
        trace[j] = jnp.broadcast_to(total_of(cov * ident), (8, 128))
    ident = jnp.where(row == lane, 1.0, 0.0)

    @pl.loop(0, 4)
    def _(pair):
        problems = [(pair * 2 + g, j) for g in range(2) for j in range(2)]
        powers, sums, scales = [], [], []
        for g, j in problems:
            gain, level = gains[g, first_freq + j], noise[first_freq + j]
            square = gain * gain
            norm = size[j, 0:1, 0:1] * (square * square)
            norm += trace[j, 0:1, 0:1] * (2.0 * square * level) + 128.0 * level * level
            scale = 1.0 / jnp.sqrt(norm)
            power = (1.0 - scale * level) * ident - (scale * square) * cov_ref[j]
            powers.append(power)
            sums.append(ident + power)
            scales.append(scale * gain)
        powers = [product(p, right_side(p)) for p in powers]
        for _ in range(NS_ITERS - 2):
            sides = [right_side(p) for p in powers]
            both = [
                product(jnp.concatenate([s, p], 0), r) for s, p, r in zip(sums, powers, sides)
            ]
            sums = [s + b[0:128] for s, b in zip(sums, both)]
            powers = [b[128:256] for b in both]
        sums = [s + product(s, right_side(p)) for s, p in zip(sums, powers)]
        for (g, j), s, scale in zip(problems, sums, scales):
            out[j, g] = (scale * product(s, cov_right[j])).astype(BF16)


def swap_kernel(mine, out, send, recv):
    x, y, z, core = place()
    partner = {"img": y * 8 + z, "grp": x * 2 + 1 - core}
    barrier = pltpu.get_barrier_semaphore()
    pl.semaphore_signal(barrier, inc=1, device_id=partner, device_id_type=MESH_ID)
    pl.semaphore_wait(barrier, 1)
    copy = pltpu.make_async_remote_copy(
        mine, out, send, recv, device_id=partner, device_id_type=MESH_ID
    )
    copy.start()
    copy.wait()


def apply_kernel(counts, packed, ids, mine, other, out, wide, filters):
    x, y, z, core = place()
    first_freq = owner_index(x, y, z) * 4
    slots = block_slots(counts, first_freq)
    lane = lanes((128, 128))

    @pl.loop(0, 8)
    def _(g):
        wide[...] = jnp.zeros_like(wide)
        for j, (offset, _) in enumerate(slots):
            value = jnp.where(core == j // 2, mine[j % 2, g].astype(F32), other[j % 2, g].astype(F32))
            shift, first = offset % 128, offset // 128
            turned = pltpu.roll(value, shift, 1)
            wide[first, pl.ds(offset, 128)] += jnp.where(lane >= shift, turned, 0.0)
            wide[first + 1, pl.ds(offset, 128)] += jnp.where(lane < shift, turned, 0.0)
        row = pl.ds(pl.multiple_of(g * 384, 384), 384)
        for t in range(3):
            filters[row, t * 128 : t * 128 + 128] = wide[t, 0:384].astype(BF16)

    @pl.loop(0, 8)
    def _(i):
        value = jnp.concatenate(chunk_slots(packed, i * 4), 1).astype(BF16)
        group = ids[pl.ds(pl.multiple_of(i * 256, 256), 256), :].astype(F32)
        pieces = []
        for g in range(8):
            mask = jnp.where(group == float(g), 1.0, 0.0).astype(BF16)
            pieces.append(value * jnp.concatenate([mask] * 3, 1))
        cleaned = jnp.dot(jnp.concatenate(pieces, 1), filters[...], preferred_element_type=F32)
        for s in range(4):
            rows = cleaned[s * 64 : s * 64 + 64]
            fold_slots(rows[:, 0:128], rows[:, 128:256], rows[:, 256:384], out.at[i * 4 + s])


def local_call(kernel, shape, dtype, in_specs, scratch, name, *operands):
    return pl.pallas_call(
        kernel,
        out_shape=jax.ShapeDtypeStruct(shape, dtype),
        in_specs=in_specs,
        out_specs=VMEM,
        scratch_shapes=scratch,
        name=name,
    )(*operands)


def remote_call(kernel, shape, dtype, scratch, collective_id, name, operand):
    return pl.pallas_call(
        kernel,
        out_shape=jax.ShapeDtypeStruct(shape, dtype),
        in_specs=[VMEM],
        out_specs=VMEM,
        scratch_shapes=scratch,
        compiler_params=pltpu.CompilerParams(collective_id=collective_id, has_side_effects=True),
        name=name,
    )(operand)


def dft_tables(angles, freqs):
    angle_index = jnp.arange(angles, dtype=jnp.int32)
    freq_index = jnp.arange(freqs, dtype=jnp.int32)
    turns = angle_index[:, None] * freq_index[None, :] % angles
    phases = turns.astype(jnp.float32) * (2.0 * math.pi / angles)
    factor = 1.0 / math.sqrt(angles)
    cosine = jnp.cos(phases) * factor
    sine = -jnp.sin(phases) * factor
    forward = jnp.concatenate([cosine, sine], 1).astype(jnp.bfloat16)
    doubling = jnp.where(freq_index == 0, 1.0, 2.0).astype(jnp.float32)
    inverse = jnp.concatenate([cosine * doubling[None, :], sine * doubling[None, :]], 1).T.astype(
        jnp.bfloat16
    )
    return (forward, inverse)


def body(images, group_ids, counts, radial_basis, ctf_gain, noise_var):
    local_images, radii, angles = images.shape
    freqs = radial_basis.shape[0]
    image_total = local_images * lax.axis_size("img") * lax.axis_size("grp")
    dma = pltpu.SemaphoreType.DMA
    forward, inverse = dft_tables(angles, freqs)
    spectrum = jnp.dot(
        images.reshape(local_images * radii, angles), forward, preferred_element_type=F32
    )
    spectrum = spectrum.astype(BF16).reshape(local_images, radii, 2, freqs)
    coeffs = jnp.einsum(
        "nrck,krp->kcnp", spectrum, radial_basis, preferred_element_type=F32
    ).astype(BF16).reshape(freqs, 64, 128)
    packed = local_call(
        pack_kernel, (32, 160, 128), BF16, [SMEM, VMEM], [pltpu.VMEM((64, 512), F32)],
        "pack", counts, coeffs,
    )
    ids = jnp.pad(group_ids, (0, 96)).reshape(1, 128)
    arrived, all_ids = exchange(packed, ids, 0)
    row_ids = jnp.broadcast_to(
        all_ids[:, 0, None, 0:32, None], (32, 2, 32, 128)
    ).astype(BF16).reshape(2048, 128)
    gram = local_call(
        gram_kernel, (4, 136, 128), F32, [SMEM, SMEM, VMEM, VMEM],
        [pltpu.VMEM((4, 512, 128), F32), pltpu.VMEM((128, 512), BF16), pltpu.VMEM((384, 128), BF16)],
        "gram", counts, ctf_gain, arrived, row_ids,
    )
    parts = remote_call(
        reduce_kernel, (4, 2, 136, 128), F32,
        [pltpu.VMEM((2, 136, 128), F32), pltpu.VMEM((2, 136, 128), F32), dma((4,)), dma((4,))],
        1, "reduce", gram,
    )
    filters = local_call(
        functools.partial(filter_kernel, image_total), (2, 8, 128, 128), BF16,
        [SMEM, SMEM, SMEM, VMEM],
        [
            pltpu.VMEM((2, 128, 128), F32), pltpu.VMEM((2, 256, 256), BF16),
            pltpu.VMEM((2, 8, 128), F32), pltpu.VMEM((2, 8, 128), F32),
        ],
        "filters", counts, ctf_gain, noise_var, parts,
    )
    partner = remote_call(swap_kernel, filters.shape, BF16, [dma, dma], 2, "swap", filters)
    cleaned = local_call(
        apply_kernel, (32, 160, 128), BF16, [SMEM, VMEM, VMEM, VMEM, VMEM],
        [pltpu.VMEM((4, 512, 128), F32), pltpu.VMEM((3072, 384), BF16)],
        "apply", counts, arrived, row_ids, filters, partner,
    )
    (returned,) = exchange(cleaned, None, 3)
    spread = local_call(
        unpack_kernel, (freqs, 64, 128), BF16, [SMEM, VMEM], [pltpu.VMEM((64, 512), F32)],
        "unpack", counts, returned,
    ).reshape(freqs, 2, local_images, 128)
    back = jnp.einsum(
        "kcnp,krp->nrck", spread, radial_basis, preferred_element_type=F32
    ).astype(BF16)
    back = back.reshape(local_images * radii, 2 * freqs)
    denoised = jnp.dot(back, inverse, preferred_element_type=F32).astype(BF16)
    return denoised.reshape(local_images, radii, angles)


def solution(mesh):
    placed = (P(("img", "grp"), None, None), P(("img", "grp")), P(), P(), P(), P())
    return jax.shard_map(
        body, mesh=mesh, in_specs=placed, out_specs=P(("img", "grp"), None, None), check_vma=False
    )
```

profile of v0, /device:TPU:1, one launch (start us, length us, event | category | flops | bytes accessed | tf_op | source)
XLA Modules:
  0.0 149.1 jit_solution(1456936329613431350)
XLA Ops:
  0.0 1.2 pad_bitcast_fusion.refs_1_
  1.3 1.1 multiply_convert_fusion.1
  2.4 1.1 multiply_convert_fusion.2
  3.5 3.5 %fusion.14 = bf16[32,8,32,128]{3,1,2,0:T(8,128)(2,1)S(1)} fusion(bf16[4096,512]{1,0:T(8,128)(2,1)} %bitcast.44, bf16[512,128]{1,0:T(8,128)(2,1)S(1)} %get-tuple-element.11, bf16[512,128]{1,0:T(8,128)(2,1)S(1)} %get-tuple-element.12), kind=kOutput, calls=%fused_computation.11 | convolution fusion | flops 1075314688 | bytes 6553600 | tf_op jit(solution)/shard_map/dot_general | solution.py:439
  7.0 0.0 copy-start
  7.1 0.5 copy.12
  7.5 1.7 %copy-done = bf16[128,128,128]{2,1,0:T(8,128)(2,1)S(1)} copy-done((bf16[128,128,128]{2,1,0:T(8,128)(2,1)S(1)}, bf16[128,128,128]{2,1,0:T(8,128)(2,1)}, u32[]{:S(2)}) %copy-start) | copy-done | bytes 4194328
  9.2 2.5 %fusion.7 = bf16[128,32,2,128]{3,1,2,0:T(8,128)(2,1)} fusion(bf16[128,128,128]{2,1,0:T(8,128)(2,1)S(1)} %copy-done, bf16[32,128,2,128]{1,0,3,2:T(8,128)(2,1)S(1)} %bitcast.41), kind=kOutput, calls=%fused_computation.10 | convolution fusion | flops 269484032 | bytes 8388608 | tf_op jit(solution)/shard_map/nrck,krp->kcnp/dot_general | solution.py:443
  11.8 8.9 %pack.1.refs_0_ = bf16[32,160,128]{2,1,0:T(8,128)(2,1)} custom-call(s32[128]{0:T(128)} %counts.9, bf16[128,64,128]{2,1,0:T(8,128)(2,1)} %bitcast.42), custom_call_target="tpu_custom_call" | custom-call | tf_op jit(solution)/shard_map/pack/pallas_call | solution.py:395
  20.7 27.3 %exchange.2 = (bf16[32,160,128]{2,1,0:T(8,128)(2,1)}, s32[32,1,128]{2,1,0:T(1,128)}) custom-call(bf16[32,160,128]{2,1,0:T(8,128)(2,1)} %pack.1.refs_0_, s32[1,128]{1,0:T(1,128)} %pad_bitcast_fusion.refs_1_), custom_call_target="tpu_custom_call" | custom-call | tf_op jit(solution)/shard_map/exchange/pallas_call | solution.py:92
  48.0 0.7 slice_convert_fusion
  48.8 0.1 broadcast_in_dim.22
  48.9 1.2 broadcast_in_dim.23.ids
  50.0 7.7 %gram.1.part = f32[4,136,128]{2,1,0:T(8,128)} custom-call(s32[128]{0:T(128)} %counts.9, f32[8,128]{1,0:T(8,128)} %gains.3, bf16[32,160,128]{2,1,0:T(8,128)(2,1)} %get-tuple-element.7.packed, bf16[2048,128]{1,0:T(8,128)(2,1)} %broadcast_in_dim.23.ids), custom_call_target="tpu_custom_call" | custom-call | tf_op jit(solution)/shard_map/gram/pallas_call | solution.py:395
  57.7 22.9 %reduce.1.parts = f32[4,2,136,128]{3,2,1,0:T(8,128)} custom-call(f32[4,136,128]{2,1,0:T(8,128)} %gram.1.part), custom_call_target="tpu_custom_call" | custom-call | tf_op jit(solution)/shard_map/reduce/pallas_call | solution.py:406
  80.6 9.6 %filters.1.mine = bf16[2,8,128,128]{3,2,1,0:T(8,128)(2,1)} custom-call(s32[128]{0:T(128)} %counts.9, f32[8,128]{1,0:T(8,128)} %gains.3, f32[128]{0:T(128)} %noise.1, f32[4,2,136,128]{3,2,1,0:T(8,128)} %reduce.1.parts), custom_call_target="tpu_custom_call" | custom-call | tf_op jit(solution)/shard_map/filters/pallas_call | solution.py:395
  90.2 4.1 %swap.1.other = bf16[2,8,128,128]{3,2,1,0:T(8,128)(2,1)} custom-call(bf16[2,8,128,128]{3,2,1,0:T(8,128)(2,1)} %filters.1.mine), custom_call_target="tpu_custom_call" | custom-call | tf_op jit(solution)/shard_map/swap/pallas_call | solution.py:406
  94.4 12.8 %apply.1.refs_0_ = bf16[32,160,128]{2,1,0:T(8,128)(2,1)} custom-call(s32[128]{0:T(128)} %counts.9, bf16[32,160,128]{2,1,0:T(8,128)(2,1)} %get-tuple-element.7.packed, bf16[2048,128]{1,0:T(8,128)(2,1)} %broadcast_in_dim.23.ids, bf16[2,8,128,128]{3,2,1,0:T(8,128)(2,1)} %filters.1.mine, bf16[2,8,128,128]{3,2,1,0:T(8,128)(2,1)} %swap.1.other), custom_call_target="tpu_custom_call" | custom-call | tf_op jit(solution)/shard_map/apply/pallas_call | solution.py:395
  107.2 23.2 %exchange.3.packed = bf16[32,160,128]{2,1,0:T(8,128)(2,1)} custom-call(bf16[32,160,128]{2,1,0:T(8,128)(2,1)} %apply.1.refs_0_), custom_call_target="tpu_custom_call" | custom-call | tf_op jit(solution)/shard_map/exchange/pallas_call | solution.py:92
  130.4 8.5 %unpack.1 = bf16[128,64,128]{2,1,0:T(8,128)(2,1)} custom-call(s32[128]{0:T(128)} %counts.9, bf16[32,160,128]{2,1,0:T(8,128)(2,1)} %exchange.3.packed), custom_call_target="tpu_custom_call" | custom-call | tf_op jit(solution)/shard_map/unpack/pallas_call | solution.py:395
  138.9 5.8 %convert_bitcast_fusion = bf16[32,128,2,128]{1,0,2,3:T(8,128)(2,1)S(1)} fusion(bf16[128,2,32,128]{3,2,1,0:T(8,128)(2,1)} %bitcast.43, bf16[128,128,128]{2,1,0:T(8,128)(2,1)} %param.9), kind=kOutput, calls=%fused_computation.9 | convolution fusion | flops 269484032 | bytes 8388608 | tf_op jit(solution)/shard_map/kcnp,krp->nrck/dot_general | solution.py:485
  144.7 0.4 copy.9
  145.1 4.0 %convolution_convert_fusion = bf16[4096,512]{1,0:T(8,128)(2,1)} fusion(bf16[32,8,32,128]{3,2,1,0:T(8,128)(2,1)S(1)} %bitcast.40, bf16[512,128]{1,0:T(8,128)(2,1)S(1)} %get-tuple-element.10, bf16[512,128]{1,0:T(8,128)(2,1)S(1)} %get-tuple-element.9), kind=kOutput, calls=%fused_computation | convolution fusion | flops 1076363264 | bytes 6553600 | tf_op jit(solution)/shard_map/dot_general | solution.py:489
  (3 shorter events, 0.0 us)
Async XLA Ops:
  7.0 2.2 %copy-start = (bf16[128,128,128]{2,1,0:T(8,128)(2,1)S(1)}, bf16[128,128,128]{2,1,0:T(8,128)(2,1)}, u32[]{:S(2)}) copy-start(bf16[128,128,128]{2,1,0:T(8,128)(2,1)} %param.9) | copy-start | bytes 12582916
where the time goes:
time: 150 us; the launch traced here: 149 us
  Pallas kernels  125 us (83%)
  matrix products  15.9 us (11%)
  local copies, waits for them, and re-layouts  5.07 us (3%)
  other arithmetic  2.97 us (2%)
    pallas_call x2, Pallas kernels, exchange(): pl.pallas_call(functools.partial(exchange_kernel, ids is not None), out_s...  50.6 us
    pallas_call x5, Pallas kernels, local_call(): pl.pallas_call(kernel, out_shape=jax.ShapeDtypeStruct(shape, dtype), in_s...  47.5 us
    pallas_call x2, Pallas kernels, remote_call(): pl.pallas_call(kernel, out_shape=jax.ShapeDtypeStruct(shape, dtype), in_s...  27 us
    dot_general x1, matrix products, body(): jnp.einsum('kcnp,krp->nrck', spread, radial_basis, preferred_element_type...  5.79 us
    dot_general x1, matrix products, body(): denoised = jnp.dot(back, inverse, preferred_element_type=F32).astype(BF16)  4.03 us
    dot_general x1, matrix products, body(): jnp.dot(images.reshape(local_images * radii, angles), forward, preferred_...  3.53 us

commit v1 on v0

--- a/solution.py
+++ b/solution.py
@@ -117,19 +117,27 @@
     return offsets
 
 
-def pack_kernel(counts, coeffs, out, wide):
+def slot_mask(lane, t, offset, count):
+    slot = lane + t * 128
+    return (slot >= offset) & (slot < offset + count)
+
+
+def pack_block(counts, coeffs, block, out):
     lane = lanes((64, 128))
-
-    @pl.loop(0, 32)
-    def _(block):
-        wide[...] = jnp.zeros_like(wide)
-        for j, (offset, count) in enumerate(block_slots(counts, block * 4)):
-            value = jnp.where(lane < count, coeffs[block * 4 + j].astype(F32), 0.0)
-            shift, first = offset % 128, offset // 128
-            turned = pltpu.roll(value, shift, 1)
-            wide[:, tile(first)] += jnp.where(lane >= shift, turned, 0.0)
-            wide[:, tile(first + 1)] += jnp.where(lane < shift, turned, 0.0)
-        fold_slots(wide[:, 0:128], wide[:, 128:256], wide[:, 256:384], out.at[block])
+    tiles = [jnp.zeros((64, 128), F32) for _ in range(3)]
+    for j, (offset, count) in enumerate(block_slots(counts, block * 4)):
+        turned = pltpu.roll(coeffs[block * 4 + j].astype(F32), offset % 128, 1)
+        tiles = [
+            jnp.where(slot_mask(lane, t, offset, count), turned, tiles[t]) for t in range(3)
+        ]
+    fold_slots(*tiles, out.at[block])
+
+
+def pack_kernel(counts, coeffs, out):
+    @pl.loop(0, 16)
+    def _(pair):
+        for half in range(2):
+            pack_block(counts, coeffs, pair * 2 + half, out)
 
 
 def fold_slots(low, middle, high, out):
@@ -147,22 +155,27 @@
     return jnp.concatenate([first, second], 0)
 
 
-def unpack_kernel(counts, packed, out, wide):
+def pick_slots(tiles, lane, offset, count):
+    picked = jnp.zeros_like(tiles[0])
+    for t in range(3):
+        picked = jnp.where(slot_mask(lane, t, offset, count), tiles[t], picked)
+    return pltpu.roll(picked, (128 - offset % 128) % 128, 1)
+
+
+def unpack_kernel(counts, packed, out):
     lane = lanes((64, 128))
-    wide[...] = jnp.zeros_like(wide)
-
-    @pl.loop(0, 32)
-    def _(block):
-        wide[:, 0:128] = packed[block, 0:64].astype(F32)
-        wide[:, 128:256] = packed[block, 64:128].astype(F32)
-        wide[:, 256:384] = unfold_slots(packed[block, 128:160])
-        for j, (offset, count) in enumerate(block_slots(counts, block * 4)):
-            shift, first = offset % 128, offset // 128
-            back = (128 - shift) % 128
-            low = pltpu.roll(wide[:, tile(first)], back, 1)
-            high = pltpu.roll(wide[:, tile(first + 1)], back, 1)
-            value = jnp.where(lane < 128 - shift, low, high)
-            out[block * 4 + j] = jnp.where(lane < count, value, 0.0).astype(BF16)
+
+    @pl.loop(0, 16)
+    def _(pair):
+        for half in range(2):
+            block = pair * 2 + half
+            tiles = [
+                packed[block, 0:64].astype(F32),
+                packed[block, 64:128].astype(F32),
+                unfold_slots(packed[block, 128:160]),
+            ]
+            for j, (offset, count) in enumerate(block_slots(counts, block * 4)):
+                out[block * 4 + j] = pick_slots(tiles, lane, offset, count).astype(BF16)
 
 
 def chunk_slots(packed, start):
@@ -226,17 +239,45 @@
     fourth, total = lax.fori_loop(0, 8, chunk, (nothing, nothing))
     row = lax.broadcasted_iota(jnp.int32, (128, 128), 0)
     lane = lanes((128, 128))
-    for j, (offset, count) in enumerate(slots):
-        shift, first = offset % 128, offset // 128
-        back = (128 - shift) % 128
-        low = pltpu.roll(gram[first, pl.ds(offset, 128)], back, 1)
-        high = pltpu.roll(gram[first + 1, pl.ds(offset, 128)], back, 1)
-        value = jnp.where(lane < 128 - shift, low, high)
-        out[j, 0:128] = jnp.where((lane < count) & (row < count), value, 0.0)
-        out[j, 128:136] = jnp.concatenate([fourth, total, jnp.zeros((6, 128), F32)], 0)
-
-
-def reduce_kernel(part, out, other, mine, send, recv):
+    squares = []
+    for offset, count in slots:
+        tiles = [gram[t, pl.ds(offset, 128)] for t in range(3)]
+        squares.append(jnp.where(row < count, pick_slots(tiles, lane, offset, count), 0.0))
+    for half in range(2):
+        upper, lower = squares[half * 2], squares[half * 2 + 1]
+        out[half, 0:128] = jnp.where(row <= lane, upper, lower)
+        diagonal = jnp.sum(jnp.where(row == lane, lower, 0.0), 0, keepdims=True)
+        out[half, 128:136] = jnp.concatenate(
+            [diagonal, fourth, total, jnp.zeros((5, 128), F32)], 0
+        )
+
+
+def split(value):
+    high = value.astype(BF16)
+    return high, (value - high.astype(F32)).astype(BF16)
+
+
+def right_side(value):
+    high, low = split(value)
+    return jnp.concatenate(
+        [jnp.concatenate([high, low], 1), jnp.concatenate([high, jnp.zeros_like(high)], 1)], 0
+    )
+
+
+def product(left, right):
+    high, low = split(left)
+    wide = jnp.dot(jnp.concatenate([high, low], 1), right, preferred_element_type=F32)
+    return wide[:, 0:128] + wide[:, 128:256]
+
+
+def total_of(value):
+    return jnp.sum(jnp.sum(value, 0, keepdims=True), 1, keepdims=True)
+
+
+def middle_kernel(
+    images, counts, gains, noise, part, out, out_other,
+    other, mine, parts, cov_ref, cov_right, size, trace, send, recv,
+):
     x, y, z, core = place()
     quarter, low = z // 2, z % 2
     partner = {"img": y * 8 + z, "grp": x * 2 + 1 - core}
@@ -247,64 +288,59 @@
     for device in [partner] + column:
         pl.semaphore_signal(barrier, inc=1, device_id=device, device_id_type=MESH_ID)
     pl.semaphore_wait(barrier, 4)
-    swap = pltpu.make_async_remote_copy(
-        part.at[pl.ds((1 - core) * 2, 2)], other, send.at[0], recv.at[0],
-        device_id=partner, device_id_type=MESH_ID,
-    )
+
+    def copy_to(source, target, index, device):
+        return pltpu.make_async_remote_copy(
+            source, target, send.at[index], recv.at[index],
+            device_id=device, device_id_type=MESH_ID,
+        )
+
+    swap = copy_to(part.at[1 - core], other, 0, partner)
     swap.start()
     swap.wait()
-    both = part[pl.ds(core * 2, 2)] + other[...]
+    both = part[core] + other[...]
     mine[...] = both
-    copies = []
-    for i, device in enumerate(column):
-        copies.append(
-            pltpu.make_async_remote_copy(
-                mine, out.at[quarter], send.at[i + 1], recv.at[i + 1],
-                device_id=device, device_id_type=MESH_ID,
-            )
-        )
+    copies = [copy_to(mine, parts.at[quarter], i + 1, d) for i, d in enumerate(column)]
     for copy in copies:
         copy.start()
-    out[quarter] = both
+    parts[quarter] = both
     for copy in copies:
         copy.wait()
-
-
-def split(value):
-    high = value.astype(BF16)
-    return high, (value - high.astype(F32)).astype(BF16)
-
-
-def right_side(value):
-    high, low = split(value)
-    return jnp.concatenate(
-        [jnp.concatenate([high, low], 1), jnp.concatenate([high, jnp.zeros_like(high)], 1)], 0
-    )
-
-
-def product(left, right):
-    high, low = split(left)
-    wide = jnp.dot(jnp.concatenate([high, low], 1), right, preferred_element_type=F32)
-    return wide[:, 0:128] + wide[:, 128:256]
-
-
-def total_of(value):
-    return jnp.sum(jnp.sum(value, 0, keepdims=True), 1, keepdims=True)
-
-
-def filter_kernel(images, counts, gains, noise, parts, out, cov_ref, cov_right, size, trace):
+    make_covariances(images, counts, parts, cov_ref, cov_right, size, trace)
+
+    def send_pair(pair):
+        groups = pl.ds(pair * 2, 2)
+        return copy_to(out.at[groups], out_other.at[groups], pair + 4, partner)
+
+    @pl.loop(0, 4)
+    def _(pair):
+        make_filters(pair, gains, noise, out, cov_ref, cov_right, size, trace)
+        send_pair(pair).start()
+
+    for pair in range(4):
+        send_pair(pair).wait()
+
+
+def make_covariances(images, counts, parts, cov_ref, cov_right, size, trace):
     x, y, z, core = place()
     first_freq = owner_index(x, y, z) * 4 + core * 2
     row = lax.broadcasted_iota(jnp.int32, (128, 128), 0)
     lane = lanes((128, 128))
     line = lanes((1, 128))
+    block = ((parts[0] + parts[1]) + parts[2]) + parts[3]
+    square = block[0:128]
+    above = jnp.where(row < lane, square, 0.0)
+    below = jnp.where(row > lane, square, 0.0)
+    grams = (
+        jnp.where(row <= lane, square, 0.0) + above.T,
+        jnp.where(row == lane, block[128:129], below) + below.T,
+    )
     for j in range(2):
-        block = ((parts[0, j] + parts[1, j]) + parts[2, j]) + parts[3, j]
         count = counts[first_freq + j]
         here = line == core * 2 + j
-        fourth = jnp.sum(jnp.where(here, block[128:129], 0.0), 1, keepdims=True)
-        total = jnp.sum(jnp.where(here, block[129:130], 0.0), 1, keepdims=True)
-        sample = block[0:128] / total
+        fourth = jnp.sum(jnp.where(here, block[129:130], 0.0), 1, keepdims=True)
+        total = jnp.sum(jnp.where(here, block[130:131], 0.0), 1, keepdims=True)
+        sample = grams[j] / total
         ident = jnp.where((row == lane) & (row < count), 1.0, 0.0)
         level = total_of(sample * ident) / count.astype(F32)
         off_level = sample - level * ident
@@ -316,46 +352,35 @@
         cov_right[j] = right_side(cov)
         size[j] = jnp.broadcast_to(total_of(cov * cov), (8, 128))
         trace[j] = jnp.broadcast_to(total_of(cov * ident), (8, 128))
-    ident = jnp.where(row == lane, 1.0, 0.0)
-
-    @pl.loop(0, 4)
-    def _(pair):
-        problems = [(pair * 2 + g, j) for g in range(2) for j in range(2)]
-        powers, sums, scales = [], [], []
-        for g, j in problems:
-            gain, level = gains[g, first_freq + j], noise[first_freq + j]
-            square = gain * gain
-            norm = size[j, 0:1, 0:1] * (square * square)
-            norm += trace[j, 0:1, 0:1] * (2.0 * square * level) + 128.0 * level * level
-            scale = 1.0 / jnp.sqrt(norm)
-            power = (1.0 - scale * level) * ident - (scale * square) * cov_ref[j]
-            powers.append(power)
-            sums.append(ident + power)
-            scales.append(scale * gain)
-        powers = [product(p, right_side(p)) for p in powers]
-        for _ in range(NS_ITERS - 2):
-            sides = [right_side(p) for p in powers]
-            both = [
-                product(jnp.concatenate([s, p], 0), r) for s, p, r in zip(sums, powers, sides)
-            ]
-            sums = [s + b[0:128] for s, b in zip(sums, both)]
-            powers = [b[128:256] for b in both]
-        sums = [s + product(s, right_side(p)) for s, p in zip(sums, powers)]
-        for (g, j), s, scale in zip(problems, sums, scales):
-            out[j, g] = (scale * product(s, cov_right[j])).astype(BF16)
-
-
-def swap_kernel(mine, out, send, recv):
+
+
+def make_filters(pair, gains, noise, out, cov_ref, cov_right, size, trace):
     x, y, z, core = place()
-    partner = {"img": y * 8 + z, "grp": x * 2 + 1 - core}
-    barrier = pltpu.get_barrier_semaphore()
-    pl.semaphore_signal(barrier, inc=1, device_id=partner, device_id_type=MESH_ID)
-    pl.semaphore_wait(barrier, 1)
-    copy = pltpu.make_async_remote_copy(
-        mine, out, send, recv, device_id=partner, device_id_type=MESH_ID
-    )
-    copy.start()
-    copy.wait()
+    first_freq = owner_index(x, y, z) * 4 + core * 2
+    ident = jnp.where(
+        lax.broadcasted_iota(jnp.int32, (128, 128), 0) == lanes((128, 128)), 1.0, 0.0
+    )
+    problems = [(pair * 2 + g, j) for g in range(2) for j in range(2)]
+    powers, sums, scales = [], [], []
+    for g, j in problems:
+        gain, level = gains[g, first_freq + j], noise[first_freq + j]
+        square = gain * gain
+        norm = size[j, 0:1, 0:1] * (square * square)
+        norm += trace[j, 0:1, 0:1] * (2.0 * square * level) + 128.0 * level * level
+        scale = 1.0 / jnp.sqrt(norm)
+        power = (1.0 - scale * level) * ident - (scale * square) * cov_ref[j]
+        powers.append(power)
+        sums.append(ident + power)
+        scales.append(scale * gain)
+    powers = [product(p, right_side(p)) for p in powers]
+    for _ in range(NS_ITERS - 2):
+        sides = [right_side(p) for p in powers]
+        both = [product(jnp.concatenate([s, p], 0), r) for s, p, r in zip(sums, powers, sides)]
+        sums = [s + b[0:128] for s, b in zip(sums, both)]
+        powers = [b[128:256] for b in both]
+    sums = [s + product(s, right_side(p)) for s, p in zip(sums, powers)]
+    for (g, j), s, scale in zip(problems, sums, scales):
+        out[g, j] = (scale * product(s, cov_right[j])).astype(BF16)
 
 
 def apply_kernel(counts, packed, ids, mine, other, out, wide, filters):
@@ -363,16 +388,17 @@
     first_freq = owner_index(x, y, z) * 4
     slots = block_slots(counts, first_freq)
     lane = lanes((128, 128))
+    wide[...] = jnp.zeros_like(wide)
 
     @pl.loop(0, 8)
     def _(g):
-        wide[...] = jnp.zeros_like(wide)
-        for j, (offset, _) in enumerate(slots):
-            value = jnp.where(core == j // 2, mine[j % 2, g].astype(F32), other[j % 2, g].astype(F32))
-            shift, first = offset % 128, offset // 128
-            turned = pltpu.roll(value, shift, 1)
-            wide[first, pl.ds(offset, 128)] += jnp.where(lane >= shift, turned, 0.0)
-            wide[first + 1, pl.ds(offset, 128)] += jnp.where(lane < shift, turned, 0.0)
+        for j, (offset, count) in enumerate(slots):
+            value = jnp.where(core == j // 2, mine[g, j % 2].astype(F32), other[g, j % 2].astype(F32))
+            turned = pltpu.roll(value, offset % 128, 1)
+            for t in range(3):
+                wide[t, pl.ds(offset, 128)] = jnp.where(
+                    slot_mask(lane, t, offset, count), turned, 0.0
+                )
         row = pl.ds(pl.multiple_of(g * 384, 384), 384)
         for t in range(3):
             filters[row, t * 128 : t * 128 + 128] = wide[t, 0:384].astype(BF16)
@@ -402,18 +428,6 @@
     )(*operands)
 
 
-def remote_call(kernel, shape, dtype, scratch, collective_id, name, operand):
-    return pl.pallas_call(
-        kernel,
-        out_shape=jax.ShapeDtypeStruct(shape, dtype),
-        in_specs=[VMEM],
-        out_specs=VMEM,
-        scratch_shapes=scratch,
-        compiler_params=pltpu.CompilerParams(collective_id=collective_id, has_side_effects=True),
-        name=name,
-    )(operand)
-
-
 def dft_tables(angles, freqs):
     angle_index = jnp.arange(angles, dtype=jnp.int32)
     freq_index = jnp.arange(freqs, dtype=jnp.int32)
@@ -444,8 +458,7 @@
         "nrck,krp->kcnp", spectrum, radial_basis, preferred_element_type=F32
     ).astype(BF16).reshape(freqs, 64, 128)
     packed = local_call(
-        pack_kernel, (32, 160, 128), BF16, [SMEM, VMEM], [pltpu.VMEM((64, 512), F32)],
-        "pack", counts, coeffs,
+        pack_kernel, (32, 160, 128), BF16, [SMEM, VMEM], [], "pack", counts, coeffs,
     )
     ids = jnp.pad(group_ids, (0, 96)).reshape(1, 128)
     arrived, all_ids = exchange(packed, ids, 0)
@@ -453,34 +466,33 @@
         all_ids[:, 0, None, 0:32, None], (32, 2, 32, 128)
     ).astype(BF16).reshape(2048, 128)
     gram = local_call(
-        gram_kernel, (4, 136, 128), F32, [SMEM, SMEM, VMEM, VMEM],
-        [pltpu.VMEM((4, 512, 128), F32), pltpu.VMEM((128, 512), BF16), pltpu.VMEM((384, 128), BF16)],
+        gram_kernel, (2, 136, 128), F32, [SMEM, SMEM, VMEM, VMEM],
+        [pltpu.VMEM((3, 512, 128), F32), pltpu.VMEM((128, 512), BF16), pltpu.VMEM((384, 128), BF16)],
         "gram", counts, ctf_gain, arrived, row_ids,
     )
-    parts = remote_call(
-        reduce_kernel, (4, 2, 136, 128), F32,
-        [pltpu.VMEM((2, 136, 128), F32), pltpu.VMEM((2, 136, 128), F32), dma((4,)), dma((4,))],
-        1, "reduce", gram,
-    )
-    filters = local_call(
-        functools.partial(filter_kernel, image_total), (2, 8, 128, 128), BF16,
-        [SMEM, SMEM, SMEM, VMEM],
-        [
+    filters = jax.ShapeDtypeStruct((8, 2, 128, 128), BF16)
+    filters, partner = pl.pallas_call(
+        functools.partial(middle_kernel, image_total),
+        out_shape=[filters, filters],
+        in_specs=[SMEM, SMEM, SMEM, VMEM],
+        out_specs=[VMEM, VMEM],
+        scratch_shapes=[
+            pltpu.VMEM((136, 128), F32), pltpu.VMEM((136, 128), F32),
+            pltpu.VMEM((4, 136, 128), F32),
             pltpu.VMEM((2, 128, 128), F32), pltpu.VMEM((2, 256, 256), BF16),
-            pltpu.VMEM((2, 8, 128), F32), pltpu.VMEM((2, 8, 128), F32),
+            pltpu.VMEM((2, 8, 128), F32), pltpu.VMEM((2, 8, 128), F32), dma((8,)), dma((8,)),
         ],
-        "filters", counts, ctf_gain, noise_var, parts,
-    )
-    partner = remote_call(swap_kernel, filters.shape, BF16, [dma, dma], 2, "swap", filters)
+        compiler_params=pltpu.CompilerParams(collective_id=1, has_side_effects=True),
+        name="middle",
+    )(counts, ctf_gain, noise_var, gram)
     cleaned = local_call(
         apply_kernel, (32, 160, 128), BF16, [SMEM, VMEM, VMEM, VMEM, VMEM],
-        [pltpu.VMEM((4, 512, 128), F32), pltpu.VMEM((3072, 384), BF16)],
+        [pltpu.VMEM((3, 512, 128), F32), pltpu.VMEM((3072, 384), BF16)],
         "apply", counts, arrived, row_ids, filters, partner,
     )
-    (returned,) = exchange(cleaned, None, 3)
+    (returned,) = exchange(cleaned, None, 2)
     spread = local_call(
-        unpack_kernel, (freqs, 64, 128), BF16, [SMEM, VMEM], [pltpu.VMEM((64, 512), F32)],
-        "unpack", counts, returned,
+        unpack_kernel, (freqs, 64, 128), BF16, [SMEM, VMEM], [], "unpack", counts, returned,
     ).reshape(freqs, 2, local_images, 128)
     back = jnp.einsum(
         "kcnp,krp->nrck", spread, radial_basis, preferred_element_type=F32

time: 150 us -> 132 us (0.88)
  Pallas kernels: 125 us -> 108 us
    pallas_call x5 -> x4, Pallas kernels: 47.5 us -> 30.7 us  [local_call(): pl.pallas_call(kernel, out_shape=jax.ShapeDtypeStruct(shape, dtype), in_s...]
    pallas_call x2 -> x1, Pallas kernels: 27 us -> 26.5 us  [body(): pl.pallas_call(functools.partial(middle_kernel, image_total), out_shape=[...]
where the time goes in v1:
time: 132 us
  Pallas kernels  108 us (82%)
  matrix products  15.9 us (12%)
  local copies, waits for them, and re-layouts  5.05 us (4%)
  other arithmetic  2.97 us (2%)
    pallas_call x2, Pallas kernels, exchange(): pl.pallas_call(functools.partial(exchange_kernel, ids is not None), out_s...  50.9 us
    pallas_call x4, Pallas kernels, local_call(): pl.pallas_call(kernel, out_shape=jax.ShapeDtypeStruct(shape, dtype), in_s...  30.7 us
    pallas_call x1, Pallas kernels, body(): pl.pallas_call(functools.partial(middle_kernel, image_total), out_shape=[...  26.5 us
    dot_general x1, matrix products, body(): jnp.einsum('kcnp,krp->nrck', spread, radial_basis, preferred_element_type...  5.79 us
    dot_general x1, matrix products, body(): denoised = jnp.dot(back, inverse, preferred_element_type=F32).astype(BF16)  4.03 us
    dot_general x1, matrix products, body(): jnp.dot(images.reshape(local_images * radii, angles), forward, preferred_...  3.53 us
    another operation x3, other arithmetic  2.96 us

profile of v1, /device:TPU:1, one launch (start us, length us, event | category | flops | bytes accessed | tf_op | source)
XLA Modules:
  0.0 132.1 jit_solution(4489482507677401293)
XLA Ops:
  0.0 1.2 pad_bitcast_fusion.refs_1_
  1.2 1.1 multiply_convert_fusion.1
  2.4 1.1 multiply_convert_fusion.2
  3.5 3.5 %fusion.14 = bf16[32,8,32,128]{3,1,2,0:T(8,128)(2,1)S(1)} fusion(bf16[4096,512]{1,0:T(8,128)(2,1)} %bitcast.44, bf16[512,128]{1,0:T(8,128)(2,1)S(1)} %get-tuple-element.15, bf16[512,128]{1,0:T(8,128)(2,1)S(1)} %get-tuple-element.16), kind=kOutput, calls=%fused_computation.11 | convolution fusion | flops 1075314688 | bytes 6553600 | tf_op jit(solution)/shard_map/dot_general | solution.py:453
  7.0 0.0 copy-start
  7.0 0.5 copy.12
  7.5 1.7 %copy-done = bf16[128,128,128]{2,1,0:T(8,128)(2,1)S(1)} copy-done((bf16[128,128,128]{2,1,0:T(8,128)(2,1)S(1)}, bf16[128,128,128]{2,1,0:T(8,128)(2,1)}, u32[]{:S(2)}) %copy-start) | copy-done | bytes 4194328
  9.2 2.5 %fusion.7 = bf16[128,32,2,128]{3,1,2,0:T(8,128)(2,1)} fusion(bf16[128,128,128]{2,1,0:T(8,128)(2,1)S(1)} %copy-done, bf16[32,128,2,128]{1,0,3,2:T(8,128)(2,1)S(1)} %bitcast.41), kind=kOutput, calls=%fused_computation.10 | convolution fusion | flops 269484032 | bytes 8388608 | tf_op jit(solution)/shard_map/nrck,krp->kcnp/dot_general | solution.py:457
  11.8 5.4 %pack.1.refs_0_ = bf16[32,160,128]{2,1,0:T(8,128)(2,1)} custom-call(s32[128]{0:T(128)} %counts.9, bf16[128,64,128]{2,1,0:T(8,128)(2,1)} %bitcast.42), custom_call_target="tpu_custom_call" | custom-call | tf_op jit(solution)/shard_map/pack/pallas_call | solution.py:421
  17.1 27.3 %exchange.2 = (bf16[32,160,128]{2,1,0:T(8,128)(2,1)}, s32[32,1,128]{2,1,0:T(1,128)}) custom-call(bf16[32,160,128]{2,1,0:T(8,128)(2,1)} %pack.1.refs_0_, s32[1,128]{1,0:T(1,128)} %pad_bitcast_fusion.refs_1_), custom_call_target="tpu_custom_call" | custom-call | tf_op jit(solution)/shard_map/exchange/pallas_call | solution.py:92
  44.5 0.7 slice_convert_fusion
  45.2 0.1 broadcast_in_dim.22
  45.3 1.2 broadcast_in_dim.23.ids
  46.5 7.6 %gram.1.part = f32[2,136,128]{2,1,0:T(8,128)} custom-call(s32[128]{0:T(128)} %counts.9, f32[8,128]{1,0:T(8,128)} %gains.3, bf16[32,160,128]{2,1,0:T(8,128)(2,1)} %get-tuple-element.9.packed, bf16[2048,128]{1,0:T(8,128)(2,1)} %broadcast_in_dim.23.ids), custom_call_target="tpu_custom_call" | custom-call | tf_op jit(solution)/shard_map/gram/pallas_call | solution.py:421
  54.1 26.5 %middle.1 = (bf16[8,2,128,128]{3,2,1,0:T(8,128)(2,1)}, bf16[8,2,128,128]{3,2,1,0:T(8,128)(2,1)}) custom-call(s32[128]{0:T(128)} %counts.9, f32[8,128]{1,0:T(8,128)} %gains.3, f32[128]{0:T(128)} %noise.1, f32[2,136,128]{2,1,0:T(8,128)} %gram.1.part), custom_call_target="tpu_custom_call" | custom-call | tf_op jit(solution)/shard_map/middle/pallas_call | solution.py:474
  80.6 12.4 %apply.1.refs_0_ = bf16[32,160,128]{2,1,0:T(8,128)(2,1)} custom-call(s32[128]{0:T(128)} %counts.9, bf16[32,160,128]{2,1,0:T(8,128)(2,1)} %get-tuple-element.9.packed, bf16[2048,128]{1,0:T(8,128)(2,1)} %broadcast_in_dim.23.ids, bf16[8,2,128,128]{3,2,1,0:T(8,128)(2,1)} %get-tuple-element.11.mine, bf16[8,2,128,128]{3,2,1,0:T(8,128)(2,1)} %get-tuple-element.12.other), custom_call_target="tpu_custom_call" | custom-call | tf_op jit(solution)/shard_map/apply/pallas_call | solution.py:421
  93.0 23.6 %exchange.3.packed = bf16[32,160,128]{2,1,0:T(8,128)(2,1)} custom-call(bf16[32,160,128]{2,1,0:T(8,128)(2,1)} %apply.1.refs_0_), custom_call_target="tpu_custom_call" | custom-call | tf_op jit(solution)/shard_map/exchange/pallas_call | solution.py:92
  116.6 5.3 %unpack.1 = bf16[128,64,128]{2,1,0:T(8,128)(2,1)} custom-call(s32[128]{0:T(128)} %counts.9, bf16[32,160,128]{2,1,0:T(8,128)(2,1)} %exchange.3.packed), custom_call_target="tpu_custom_call" | custom-call | tf_op jit(solution)/shard_map/unpack/pallas_call | solution.py:421
  121.9 5.8 %convert_bitcast_fusion = bf16[32,128,2,128]{1,0,2,3:T(8,128)(2,1)S(1)} fusion(bf16[128,2,32,128]{3,2,1,0:T(8,128)(2,1)} %bitcast.43, bf16[128,128,128]{2,1,0:T(8,128)(2,1)} %param.9), kind=kOutput, calls=%fused_computation.9 | convolution fusion | flops 269484032 | bytes 8388608 | tf_op jit(solution)/shard_map/kcnp,krp->nrck/dot_general | solution.py:497
  127.7 0.4 copy.9
  128.1 4.0 %convolution_convert_fusion = bf16[4096,512]{1,0:T(8,128)(2,1)} fusion(bf16[32,8,32,128]{3,2,1,0:T(8,128)(2,1)S(1)} %bitcast.40, bf16[512,128]{1,0:T(8,128)(2,1)S(1)} %get-tuple-element.14, bf16[512,128]{1,0:T(8,128)(2,1)S(1)} %get-tuple-element.13), kind=kOutput, calls=%fused_computation | convolution fusion | flops 1076363264 | bytes 6553600 | tf_op jit(solution)/shard_map/dot_general | solution.py:501
  (3 shorter events, 0.0 us)
Async XLA Ops:
  7.0 2.2 %copy-start = (bf16[128,128,128]{2,1,0:T(8,128)(2,1)S(1)}, bf16[128,128,128]{2,1,0:T(8,128)(2,1)}, u32[]{:S(2)}) copy-start(bf16[128,128,128]{2,1,0:T(8,128)(2,1)} %param.9) | copy-start | bytes 12582916

commit v2 on v1

v2 whole, which is shorter than its diff:
```python
import functools
import math

import jax
import jax.numpy as jnp
from jax import lax
from jax.experimental import pallas as pl
from jax.experimental.pallas import tpu as pltpu
from jax.sharding import PartitionSpec as P

NS_ITERS = 7
SIDE = 4
MESH_ID = pl.DeviceIdType.MESH
VMEM = pl.BlockSpec(memory_space=pltpu.VMEM)
SMEM = pl.BlockSpec(memory_space=pltpu.SMEM)
F32 = jnp.float32
BF16 = jnp.bfloat16


def place():
    img = lax.axis_index("img")
    grp = lax.axis_index("grp")
    return grp // 2, img // 8, img % 8, grp % 2


def owner_index(x, y, z):
    return x * 8 + y * 2 + z % 2


def step_of(i):
    turn = i % 4
    return (turn + 1) % 4, (i // 4 + turn + 2) % 4, 1 - i // 16


def peer_of(i, sign):
    x, y, z, core = place()
    a, b, c = step_of(i)
    px, py = (x + SIDE + sign * a) % SIDE, (y + SIDE + sign * b) % SIDE
    pz = z // 2 * 2 + (z + c) % 2
    return {"img": py * 8 + pz, "grp": px * 2 + core}, owner_index(px, py, pz)


def lanes(shape):
    return lax.broadcasted_iota(jnp.int32, shape, len(shape) - 1)


def tile(index):
    return pl.ds(pl.multiple_of(index * 128, 128), 128)


def block_slots(counts, first):
    offsets, offset = [], 0
    for j in range(4):
        count = counts[first + j]
        offsets.append((offset, count))
        offset = offset + count
    return offsets


def slot_mask(lane, t, offset, count):
    slot = lane + t * 128
    return (slot >= offset) & (slot < offset + count)


def pack_block(counts, coeffs, block, out):
    lane = lanes((64, 128))
    tiles = [jnp.zeros((64, 128), F32) for _ in range(3)]
    for j, (offset, count) in enumerate(block_slots(counts, block * 4)):
        turned = pltpu.roll(coeffs[block * 4 + j].astype(F32), offset % 128, 1)
        tiles = [
            jnp.where(slot_mask(lane, t, offset, count), turned, tiles[t]) for t in range(3)
        ]
    fold_slots(*tiles, out.at[block])


def fold_slots(low, middle, high, out):
    out[0:64] = low.astype(BF16)
    out[64:128] = middle.astype(BF16)
    lane = lanes((32, 128))
    out[128:160] = jnp.where(lane < 64, high[0:32], pltpu.roll(high[32:64], 64, 1)).astype(BF16)


def unfold_slots(high):
    lane = lanes((32, 128))
    high = high.astype(F32)
    first = jnp.where(lane < 64, high, 0.0)
    second = jnp.where(lane < 64, pltpu.roll(high, 64, 1), 0.0)
    return jnp.concatenate([first, second], 0)


def pick_slots(tiles, lane, offset, count):
    picked = jnp.zeros_like(tiles[0])
    for t in range(3):
        picked = jnp.where(slot_mask(lane, t, offset, count), tiles[t], picked)
    return pltpu.roll(picked, (128 - offset % 128) % 128, 1)


def unpack_block(counts, packed, block, out):
    lane = lanes((64, 128))
    tiles = [
        packed[block, 0:64].astype(F32),
        packed[block, 64:128].astype(F32),
        unfold_slots(packed[block, 128:160]),
    ]
    for j, (offset, count) in enumerate(block_slots(counts, block * 4)):
        out[block * 4 + j] = pick_slots(tiles, lane, offset, count).astype(BF16)


def chunk_slots(packed, sources):
    rows = [packed[s] for s in sources]
    low = jnp.concatenate([r[0:64] for r in rows], 0).astype(F32)
    middle = jnp.concatenate([r[64:128] for r in rows], 0).astype(F32)
    high = jnp.concatenate([unfold_slots(r[128:160]) for r in rows], 0)
    return low, middle, high


def chunk_groups(ids, sources):
    rows = []
    for s in sources:
        column = pltpu.roll(ids[...], (128 - s) % 128, 1)[:, 0:1]
        rows += [jnp.broadcast_to(column, (32, 128))] * 2
    return jnp.concatenate(rows, 0)


def make_tables(slots, gains, first_freq, gram, table, member):
    gram[...] = jnp.zeros_like(gram)
    row = lax.broadcasted_iota(jnp.int32, (8, 512), 0)
    lane = lanes((8, 512))
    slot_gain = jnp.zeros((8, 512), F32)
    for j, (offset, count) in enumerate(slots):
        column = jnp.zeros((8, 512), F32)
        for g in range(8):
            column = jnp.where(row == g, gains[g, first_freq + j], column)
        here = ((lane >= offset) & (lane < offset + count)) | (lane == 384 + j)
        slot_gain = jnp.where(here, column, slot_gain)
    high = slot_gain.astype(BF16).astype(F32)
    middle = (slot_gain - high).astype(BF16).astype(F32)
    low = slot_gain - high - middle
    table[...] = jnp.concatenate([high, middle, low, jnp.zeros((104, 512), F32)], 0).astype(BF16)
    row = lax.broadcasted_iota(jnp.int32, (384, 128), 0)
    lane = lanes((384, 128))
    inside = jnp.zeros((384, 128), F32)
    for j, (offset, count) in enumerate(slots):
        inside = jnp.where((lane == j) & (row >= offset) & (row < offset + count), 1.0, inside)
    member[...] = inside.astype(BF16)


def add_chunk(packed, ids, sources, gram, table, member, sums):
    fourth, total = sums
    lane = lanes((256, 128))
    wanted = jnp.where(lane < 24, lane % 8, -1).astype(F32)
    value = jnp.concatenate(chunk_slots(packed, sources), 1)
    onehot = jnp.where(chunk_groups(ids, sources) == wanted, 1.0, 0.0).astype(BF16)
    gain = jnp.dot(onehot, table[...], preferred_element_type=F32)
    scaled = (value * gain[:, 0:384]).astype(BF16)
    products = lax.dot_general(
        scaled, scaled, (((0,), (0,)), ((), ())), preferred_element_type=F32
    )
    for t in range(3):
        gram[t, 0:384] += products[:, t * 128 : t * 128 + 128]
    square = value * value
    upper = square.astype(BF16)
    lower = (square - upper.astype(F32)).astype(BF16)
    norms = jnp.dot(upper, member[...], preferred_element_type=F32)
    norms += jnp.dot(lower, member[...], preferred_element_type=F32)
    weight = gain[:, 384:512] * gain[:, 384:512]
    fourth += jnp.sum(weight * norms * norms, 0, keepdims=True)
    total += jnp.sum(weight, 0, keepdims=True)
    return fourth, total


def gather_grams(slots, gram, sums, out):
    fourth, total = sums
    row = lax.broadcasted_iota(jnp.int32, (128, 128), 0)
    lane = lanes((128, 128))
    squares = []
    for offset, count in slots:
        tiles = [gram[t, pl.ds(offset, 128)] for t in range(3)]
        squares.append(jnp.where(row < count, pick_slots(tiles, lane, offset, count), 0.0))
    for half in range(2):
        upper, lower = squares[half * 2], squares[half * 2 + 1]
        out[half, 0:128] = jnp.where(row <= lane, upper, lower)
        diagonal = jnp.sum(jnp.where(row == lane, lower, 0.0), 0, keepdims=True)
        out[half, 128:136] = jnp.concatenate(
            [diagonal, fourth, total, jnp.zeros((5, 128), F32)], 0
        )


def split(value):
    high = value.astype(BF16)
    return high, (value - high.astype(F32)).astype(BF16)


def right_side(value):
    high, low = split(value)
    return jnp.concatenate(
        [jnp.concatenate([high, low], 1), jnp.concatenate([high, jnp.zeros_like(high)], 1)], 0
    )


def product(left, right):
    high, low = split(left)
    wide = jnp.dot(jnp.concatenate([high, low], 1), right, preferred_element_type=F32)
    return wide[:, 0:128] + wide[:, 128:256]


def total_of(value):
    return jnp.sum(jnp.sum(value, 0, keepdims=True), 1, keepdims=True)


def main_kernel(
    images, counts, gains, noise, coeffs, my_ids, out,
    packed, arrived, cleaned, returned, all_ids, ids, gram, table, member,
    part, other, mine, parts, cov_ref, cov_right, size, trace,
    my_filters, other_filters, shifted, filters,
    local, send, recv, send_ids, recv_ids, send_back, recv_back, send_sum, recv_sum,
):
    x, y, z, core = place()
    me = owner_index(x, y, z)
    quarter, low = z // 2, z % 2
    slots = block_slots(counts, me * 4)
    partner = {"img": y * 8 + z, "grp": x * 2 + 1 - core}
    column = []
    for step in (2, 1, 3):
        column.append({"img": y * 8 + (quarter + step) % 4 * 2 + low, "grp": x * 2 + core})
    barrier = pltpu.get_barrier_semaphore()
    for device in [peer_of(i, 1)[0] for i in range(31)] + [partner] + column:
        pl.semaphore_signal(barrier, inc=1, device_id=device, device_id_type=MESH_ID)

    def remote(source, target, sent, received, device):
        return pltpu.make_async_remote_copy(
            source, target, sent, received, device_id=device, device_id_type=MESH_ID
        )

    def data_copy(i):
        device, index = peer_of(i, 1)
        return remote(packed.at[index], arrived.at[me], send.at[i], recv.at[i], device)

    def ids_copy(i):
        return remote(my_ids, all_ids.at[me], send_ids.at[i], recv_ids.at[i], peer_of(i, 1)[0])

    def back_copy(i):
        device, index = peer_of(i, 1)
        return remote(cleaned.at[index], returned.at[me], send_back.at[i], recv_back.at[i], device)

    def sum_copy(source, target, i, device):
        return remote(source, target, send_sum.at[i], recv_sum.at[i], device)

    @pl.loop(0, 20)
    def _(i):
        pack_block(counts, coeffs, peer_of(i, 1)[1], packed)

    make_tables(slots, gains, me * 4, gram, table, member)
    pl.semaphore_wait(barrier, 35)

    @pl.loop(0, 31)
    def _(i):
        ids_copy(i).start()

    @pl.loop(0, 20)
    def _(i):
        data_copy(i).start()

    @pl.loop(20, 32)
    def _(i):
        pack_block(counts, coeffs, peer_of(i, 1)[1], packed)

        @pl.when(i < 31)
        def _():
            data_copy(i).start()

    own = pltpu.make_async_copy(packed.at[me], arrived.at[me], local.at[0])
    own.start()
    own_ids = pltpu.make_async_copy(my_ids, all_ids.at[me], local.at[1])
    own_ids.start()
    own_ids.wait()

    @pl.loop(0, 31)
    def _(i):
        ids_copy(i).wait()

    wide = jnp.concatenate([all_ids[s] for s in range(32)], 0).astype(F32)
    ids[...] = jnp.concatenate([wide, jnp.zeros((96, 128), F32)], 0).T[0:32]
    own.wait()

    def chunk(m, sums):
        sources = []
        for s in range(4):
            i = m * 4 + s
            if s < 3:
                data_copy(i).wait_recv()
            else:

                @pl.when(i < 31)
                def _():
                    data_copy(i).wait_recv()

            sources.append(peer_of(i, -1)[1])
        return add_chunk(arrived, ids, sources, gram, table, member, sums)

    nothing = jnp.zeros((1, 128), F32)
    gather_grams(slots, gram, lax.fori_loop(0, 8, chunk, (nothing, nothing)), part)

    swap = sum_copy(part.at[1 - core], other, 0, partner)
    swap.start()
    swap.wait()
    both = part[core] + other[...]
    mine[...] = both
    copies = [sum_copy(mine, parts.at[quarter], i + 1, d) for i, d in enumerate(column)]
    for copy in copies:
        copy.start()
    parts[quarter] = both
    for copy in copies:
        copy.wait()
    make_covariances(images, counts, parts, cov_ref, cov_right, size, trace)

    def send_pair(pair):
        groups = pl.ds(pair * 2, 2)
        return sum_copy(my_filters.at[groups], other_filters.at[groups], pair + 4, partner)

    @pl.loop(0, 4)
    def _(pair):
        make_filters(pair, gains, noise, my_filters, cov_ref, cov_right, size, trace)
        send_pair(pair).start()

    shifted[...] = jnp.zeros_like(shifted)

    @pl.loop(0, 4)
    def _(pair):
        send_pair(pair).wait()
        for half in range(2):
            place_filters(slots, pair * 2 + half, my_filters, other_filters, shifted, filters)

    @pl.loop(0, 8)
    def _(m):
        apply_chunk(arrived, ids, [peer_of(m * 4 + s, 1)[1] for s in range(4)], filters, cleaned)
        for s in range(4):
            i = m * 4 + s
            if s < 3:
                back_copy(i).start()
            else:

                @pl.when(i < 31)
                def _():
                    back_copy(i).start()

    unpack_block(counts, cleaned, me, out)

    @pl.loop(0, 31)
    def _(i):
        back_copy(i).wait_recv()
        unpack_block(counts, returned, peer_of(i, -1)[1], out)

    @pl.loop(0, 31)
    def _(i):
        data_copy(i).wait_send()
        back_copy(i).wait_send()


def make_covariances(images, counts, parts, cov_ref, cov_right, size, trace):
    x, y, z, core = place()
    first_freq = owner_index(x, y, z) * 4 + core * 2
    row = lax.broadcasted_iota(jnp.int32, (128, 128), 0)
    lane = lanes((128, 128))
    line = lanes((1, 128))
    block = ((parts[0] + parts[1]) + parts[2]) + parts[3]
    square = block[0:128]
    above = jnp.where(row < lane, square, 0.0)
    below = jnp.where(row > lane, square, 0.0)
    grams = (
        jnp.where(row <= lane, square, 0.0) + above.T,
        jnp.where(row == lane, block[128:129], below) + below.T,
    )
    for j in range(2):
        count = counts[first_freq + j]
        here = line == core * 2 + j
        fourth = jnp.sum(jnp.where(here, block[129:130], 0.0), 1, keepdims=True)
        total = jnp.sum(jnp.where(here, block[130:131], 0.0), 1, keepdims=True)
        sample = grams[j] / total
        ident = jnp.where((row == lane) & (row < count), 1.0, 0.0)
        level = total_of(sample * ident) / count.astype(F32)
        off_level = sample - level * ident
        spread = total_of(off_level * off_level)
        excess = (fourth / total - total_of(sample * sample)) / (2.0 * images)
        weight = excess / (excess + spread)
        cov = (1.0 - weight) * sample + (weight * level) * ident
        cov_ref[j] = cov
        cov_right[j] = right_side(cov)
        size[j] = jnp.broadcast_to(total_of(cov * cov), (8, 128))
        trace[j] = jnp.broadcast_to(total_of(cov * ident), (8, 128))


def make_filters(pair, gains, noise, out, cov_ref, cov_right, size, trace):
    x, y, z, core = place()
    first_freq = owner_index(x, y, z) * 4 + core * 2
    ident = jnp.where(
        lax.broadcasted_iota(jnp.int32, (128, 128), 0) == lanes((128, 128)), 1.0, 0.0
    )
    problems = [(pair * 2 + g, j) for g in range(2) for j in range(2)]
    powers, sums, scales = [], [], []
    for g, j in problems:
        gain, level = gains[g, first_freq + j], noise[first_freq + j]
        square = gain * gain
        norm = size[j, 0:1, 0:1] * (square * square)
        norm += trace[j, 0:1, 0:1] * (2.0 * square * level) + 128.0 * level * level
        scale = 1.0 / jnp.sqrt(norm)
        power = (1.0 - scale * level) * ident - (scale * square) * cov_ref[j]
        powers.append(power)
        sums.append(ident + power)
        scales.append(scale * gain)
    powers = [product(p, right_side(p)) for p in powers]
    for _ in range(NS_ITERS - 2):
        sides = [right_side(p) for p in powers]
        both = [product(jnp.concatenate([s, p], 0), r) for s, p, r in zip(sums, powers, sides)]
        sums = [s + b[0:128] for s, b in zip(sums, both)]
        powers = [b[128:256] for b in both]
    sums = [s + product(s, right_side(p)) for s, p in zip(sums, powers)]
    for (g, j), s, scale in zip(problems, sums, scales):
        out[g, j] = (scale * product(s, cov_right[j])).astype(BF16)


def place_filters(slots, g, mine, other, shifted, filters):
    core = place()[3]
    lane = lanes((128, 128))
    tiles = [[jnp.zeros((128, 128), F32)] * 3 for _ in range(3)]
    for j, (offset, count) in enumerate(slots):
        value = jnp.where(core == j // 2, mine[g, j % 2].astype(F32), other[g, j % 2].astype(F32))
        shifted[j, 128:256] = pltpu.roll(value, offset % 128, 1)
        for r in range(3):
            start = jnp.clip(r * 128 + 128 - offset, 0, 256)
            rows = shifted[j, pl.ds(start, 128)]
            for t in range(3):
                tiles[r][t] += jnp.where(slot_mask(lane, t, offset, count), rows, 0.0)
    for r in range(3):
        row = pl.ds(pl.multiple_of(g * 384 + r * 128, 128), 128)
        for t in range(3):
            filters[row, t * 128 : t * 128 + 128] = tiles[r][t].astype(BF16)


def apply_chunk(packed, ids, sources, filters, out):
    value = jnp.concatenate(chunk_slots(packed, sources), 1).astype(BF16)
    group = chunk_groups(ids, sources)
    pieces = []
    for g in range(8):
        mask = jnp.where(group == float(g), 1.0, 0.0).astype(BF16)
        pieces.append(value * jnp.concatenate([mask] * 3, 1))
    cleaned = jnp.dot(jnp.concatenate(pieces, 1), filters[...], preferred_element_type=F32)
    for s, source in enumerate(sources):
        rows = cleaned[s * 64 : s * 64 + 64]
        fold_slots(rows[:, 0:128], rows[:, 128:256], rows[:, 256:384], out.at[source])


def dft_tables(angles, freqs):
    angle_index = jnp.arange(angles, dtype=jnp.int32)
    freq_index = jnp.arange(freqs, dtype=jnp.int32)
    turns = angle_index[:, None] * freq_index[None, :] % angles
    phases = turns.astype(jnp.float32) * (2.0 * math.pi / angles)
    factor = 1.0 / math.sqrt(angles)
    cosine = jnp.cos(phases) * factor
    sine = -jnp.sin(phases) * factor
    forward = jnp.concatenate([cosine, sine], 1).astype(jnp.bfloat16)
    doubling = jnp.where(freq_index == 0, 1.0, 2.0).astype(jnp.float32)
    inverse = jnp.concatenate([cosine * doubling[None, :], sine * doubling[None, :]], 1).T.astype(
        jnp.bfloat16
    )
    return (forward, inverse)


def body(images, group_ids, counts, radial_basis, ctf_gain, noise_var):
    local_images, radii, angles = images.shape
    freqs = radial_basis.shape[0]
    image_total = local_images * lax.axis_size("img") * lax.axis_size("grp")
    dma = pltpu.SemaphoreType.DMA
    forward, inverse = dft_tables(angles, freqs)
    spectrum = jnp.dot(
        images.reshape(local_images * radii, angles), forward, preferred_element_type=F32
    )
    spectrum = spectrum.astype(BF16).reshape(local_images, radii, 2, freqs)
    coeffs = jnp.einsum(
        "nrck,krp->kcnp", spectrum, radial_basis, preferred_element_type=F32
    ).astype(BF16).reshape(freqs, 64, 128)
    ids = jnp.pad(group_ids, (0, 96)).reshape(1, 128)
    data = pltpu.VMEM((32, 160, 128), BF16)
    sums = pltpu.VMEM((136, 128), F32)
    pairs = pltpu.VMEM((8, 2, 128, 128), BF16)
    small = pltpu.VMEM((2, 8, 128), F32)
    spread = pl.pallas_call(
        functools.partial(main_kernel, image_total),
        out_shape=jax.ShapeDtypeStruct((freqs, 64, 128), BF16),
        in_specs=[SMEM, SMEM, SMEM, VMEM, VMEM],
        out_specs=VMEM,
        scratch_shapes=[
            data, data, data, data,
            pltpu.VMEM((32, 1, 128), jnp.int32), pltpu.VMEM((32, 128), F32),
            pltpu.VMEM((3, 512, 128), F32), pltpu.VMEM((128, 512), BF16),
            pltpu.VMEM((384, 128), BF16),
            pltpu.VMEM((2, 136, 128), F32), sums, sums, pltpu.VMEM((4, 136, 128), F32),
            pltpu.VMEM((2, 128, 128), F32), pltpu.VMEM((2, 256, 256), BF16), small, small,
            pairs, pairs, pltpu.VMEM((4, 384, 128), F32), pltpu.VMEM((3072, 384), BF16),
            dma((2,)), dma((31,)), dma((31,)), dma((31,)), dma((31,)), dma((31,)), dma((31,)),
            dma((8,)), dma((8,)),
        ],
        compiler_params=pltpu.CompilerParams(collective_id=0, has_side_effects=True),
        name="denoise",
    )(counts, ctf_gain, noise_var, coeffs, ids).reshape(freqs, 2, local_images, 128)
    back = jnp.einsum(
        "kcnp,krp->nrck", spread, radial_basis, preferred_element_type=F32
    ).astype(BF16)
    back = back.reshape(local_images * radii, 2 * freqs)
    denoised = jnp.dot(back, inverse, preferred_element_type=F32).astype(BF16)
    return denoised.reshape(local_images, radii, angles)


def solution(mesh):
    placed = (P(("img", "grp"), None, None), P(("img", "grp")), P(), P(), P(), P())
    return jax.shard_map(
        body, mesh=mesh, in_specs=placed, out_specs=P(("img", "grp"), None, None), check_vma=False
    )
```

time: 132 us -> 103 us (0.78)
  Pallas kernels: 108 us -> 80.8 us
  local copies, waits for them, and re-layouts: 5.05 us -> 3.69 us
    pallas_call x7 -> x1, Pallas kernels: 108 us -> 80.8 us  [body(): pl.pallas_call(functools.partial(main_kernel, image_total), out_shape=jax...]
    another operation x3 -> x2, other arithmetic: 2.96 us -> 2.23 us
where the time goes in v2:
time: 103 us
  Pallas kernels  80.8 us (78%)
  matrix products  15.9 us (15%)
  local copies, waits for them, and re-layouts  3.69 us (4%)
  other arithmetic  2.24 us (2%)
    pallas_call x1, Pallas kernels, body(): pl.pallas_call(functools.partial(main_kernel, image_total), out_shape=jax...  80.8 us
    dot_general x1, matrix products, body(): jnp.einsum('kcnp,krp->nrck', spread, radial_basis, preferred_element_type...  5.79 us
    dot_general x1, matrix products, body(): denoised = jnp.dot(back, inverse, preferred_element_type=F32).astype(BF16)  4.03 us
    dot_general x1, matrix products, body(): jnp.dot(images.reshape(local_images * radii, angles), forward, preferred_...  3.53 us
    dot_general x1, matrix products, body(): jnp.einsum('nrck,krp->kcnp', spectrum, radial_basis, preferred_element_ty...  2.55 us
    another operation x2, other arithmetic  2.23 us
    unnamed x3, local copies, waits for them, and re-layouts  2.18 us

profile of v2, /device:TPU:1, one launch (start us, length us, event | category | flops | bytes accessed | tf_op | source)
XLA Modules:
  0.0 102.7 jit_solution(12020559418870179473)
XLA Ops:
  0.0 1.1 %pad_bitcast_fusion.my_ids = s32[1,128]{1,0:T(1,128)} fusion(s32[32]{0:T(128)} %param.7), kind=kLoop, calls=%fused_computation.35 | loop fusion | bytes 640 | tf_op jit(solution)/shard_map/reshape | solution.py:482
  1.1 1.1 %multiply_convert_fusion.1 = (bf16[512,128]{1,0:T(8,128)(2,1)S(1)}, bf16[512,128]{1,0:T(8,128)(2,1)S(1)}) fusion(f32[128]{0:T(128)S(1)} %fusion.28), kind=kLoop, calls=%fused_computation.25 | loop fusion | flops 1245184 | bytes 262656 | tf_op jit(solution)/shard_map/convert
  2.3 1.1 %multiply_convert_fusion.2 = (bf16[512,128]{1,0:T(8,128)(2,1)S(1)}, bf16[512,128]{1,0:T(8,128)(2,1)S(1)}) fusion(), kind=kLoop, calls=%fused_computation.26 | loop fusion | flops 1245184 | bytes 262144 | tf_op jit(solution)/shard_map/convert.3
  3.4 3.5 %fusion.14 = bf16[32,8,32,128]{3,1,2,0:T(8,128)(2,1)S(1)} fusion(bf16[4096,512]{1,0:T(8,128)(2,1)} %bitcast.41, bf16[512,128]{1,0:T(8,128)(2,1)S(1)} %get-tuple-element.7, bf16[512,128]{1,0:T(8,128)(2,1)S(1)} %get-tuple-element.8), kind=kOutput, calls=%fused_computation.11 | convolution fusion | flops 1075314688 | bytes 6553600 | tf_op jit(solution)/shard_map/dot_general | solution.py:475
  6.9 0.0 copy-start
  6.9 0.5 copy.11
  7.4 1.7 %copy-done = bf16[128,128,128]{2,1,0:T(8,128)(2,1)S(1)} copy-done((bf16[128,128,128]{2,1,0:T(8,128)(2,1)S(1)}, bf16[128,128,128]{2,1,0:T(8,128)(2,1)}, u32[]{:S(2)}) %copy-start) | copy-done | bytes 4194328
  9.1 2.5 %fusion.7 = bf16[128,32,2,128]{3,1,2,0:T(8,128)(2,1)} fusion(bf16[128,128,128]{2,1,0:T(8,128)(2,1)S(1)} %copy-done, bf16[32,128,2,128]{1,0,3,2:T(8,128)(2,1)S(1)} %bitcast.40), kind=kOutput, calls=%fused_computation.10 | convolution fusion | flops 269484032 | bytes 8388608 | tf_op jit(solution)/shard_map/nrck,krp->kcnp/dot_general | solution.py:479
  11.7 80.8 %denoise.1 = bf16[128,64,128]{2,1,0:T(8,128)(2,1)} custom-call(s32[128]{0:T(128)} %counts.1, f32[8,128]{1,0:T(8,128)} %gains.1, f32[128]{0:T(128)} %noise.1, bf16[128,64,128]{2,1,0:T(8,128)(2,1)} %bitcast.38, s32[1,128]{1,0:T(1,128)} %pad_bitcast_fusion.my_ids), custom_call_target="tpu_custom_call" | custom-call | tf_op jit(solution)/shard_map/denoise/pallas_call | solution.py:487
  92.5 5.8 %convert_bitcast_fusion = bf16[32,128,2,128]{1,0,2,3:T(8,128)(2,1)S(1)} fusion(bf16[128,2,32,128]{3,2,1,0:T(8,128)(2,1)} %bitcast.39, bf16[128,128,128]{2,1,0:T(8,128)(2,1)} %param.9), kind=kOutput, calls=%fused_computation.9 | convolution fusion | flops 269484032 | bytes 8388608 | tf_op jit(solution)/shard_map/kcnp,krp->nrck/dot_general | solution.py:506
  98.3 0.4 copy.9
  98.7 4.0 %convolution_convert_fusion = bf16[4096,512]{1,0:T(8,128)(2,1)} fusion(bf16[32,8,32,128]{3,2,1,0:T(8,128)(2,1)S(1)} %bitcast.37, bf16[512,128]{1,0:T(8,128)(2,1)S(1)} %get-tuple-element.6, bf16[512,128]{1,0:T(8,128)(2,1)S(1)} %get-tuple-element.5), kind=kOutput, calls=%fused_computation | convolution fusion | flops 1076363264 | bytes 6553600 | tf_op jit(solution)/shard_map/dot_general | solution.py:510
  (1 shorter events, 0.0 us)
Async XLA Ops:
  6.9 2.2 %copy-start = (bf16[128,128,128]{2,1,0:T(8,128)(2,1)S(1)}, bf16[128,128,128]{2,1,0:T(8,128)(2,1)}, u32[]{:S(2)}) copy-start(bf16[128,128,128]{2,1,0:T(8,128)(2,1)} %param.9) | copy-start | bytes 12582916

commit v3 on v2

--- a/solution.py
+++ b/solution.py
@@ -3,6 +3,7 @@
 
 import jax
 import jax.numpy as jnp
+import numpy as np
 from jax import lax
 from jax.experimental import pallas as pl
 from jax.experimental.pallas import tpu as pltpu
@@ -62,11 +63,16 @@
     return (slot >= offset) & (slot < offset + count)
 
 
-def pack_block(counts, coeffs, block, out):
+def pack_block(counts, spectrum, basis, block, out):
     lane = lanes((64, 128))
     tiles = [jnp.zeros((64, 128), F32) for _ in range(3)]
     for j, (offset, count) in enumerate(block_slots(counts, block * 4)):
-        turned = pltpu.roll(coeffs[block * 4 + j].astype(F32), offset % 128, 1)
+        freq = block * 4 + j
+        rows = [spectrum[pl.ds(pl.multiple_of((c * 128 + freq) * 32, 32), 32), :] for c in range(2)]
+        coeffs = jnp.dot(
+            jnp.concatenate(rows, 0).astype(BF16), basis[freq], preferred_element_type=F32
+        )
+        turned = pltpu.roll(coeffs, offset % 128, 1)
         tiles = [
             jnp.where(slot_mask(lane, t, offset, count), turned, tiles[t]) for t in range(3)
         ]
@@ -95,7 +101,7 @@
     return pltpu.roll(picked, (128 - offset % 128) % 128, 1)
 
 
-def unpack_block(counts, packed, block, out):
+def unpack_block(counts, packed, basis, block, out):
     lane = lanes((64, 128))
     tiles = [
         packed[block, 0:64].astype(F32),
@@ -103,7 +109,13 @@
         unfold_slots(packed[block, 128:160]),
     ]
     for j, (offset, count) in enumerate(block_slots(counts, block * 4)):
-        out[block * 4 + j] = pick_slots(tiles, lane, offset, count).astype(BF16)
+        freq = block * 4 + j
+        cleaned = pick_slots(tiles, lane, offset, count).astype(BF16)
+        back = lax.dot_general(
+            cleaned, basis[freq], (((1,), (1,)), ((), ())), preferred_element_type=F32
+        ).astype(BF16)
+        for c in range(2):
+            out[c * 128 + freq] = back[c * 32 : c * 32 + 32]
 
 
 def chunk_slots(packed, sources):
@@ -209,16 +221,27 @@
 
 
 def main_kernel(
-    images, counts, gains, noise, coeffs, my_ids, out,
-    packed, arrived, cleaned, returned, all_ids, ids, gram, table, member,
+    image_total, counts, gains, noise, images, basis_in, forward, my_ids, out,
+    pixels, spectrum, basis, packed, arrived, cleaned, returned, all_ids, ids, gram, table, member,
     part, other, mine, parts, cov_ref, cov_right, size, trace,
     my_filters, other_filters, shifted, filters,
-    local, send, recv, send_ids, recv_ids, send_back, recv_back, send_sum, recv_sum,
+    local, load, load_basis, send, recv, send_ids, recv_ids, send_back, recv_back, send_sum, recv_sum,
 ):
     x, y, z, core = place()
     me = owner_index(x, y, z)
     quarter, low = z // 2, z % 2
     slots = block_slots(counts, me * 4)
+
+    def image_copy(m):
+        rows = pl.ds(pl.multiple_of(m * 512, 512), 512)
+        return pltpu.make_async_copy(images.at[rows], pixels.at[rows], load.at[m])
+
+    def basis_copy(i):
+        freqs = pl.ds(peer_of(i, 1)[1] * 4, 4)
+        return pltpu.make_async_copy(basis_in.at[freqs], basis.at[freqs], load_basis.at[i])
+
+    for m in range(8):
+        image_copy(m).start()
     partner = {"img": y * 8 + z, "grp": x * 2 + 1 - core}
     column = []
     for step in (2, 1, 3):
@@ -246,28 +269,41 @@
     def sum_copy(source, target, i, device):
         return remote(source, target, send_sum.at[i], recv_sum.at[i], device)
 
-    @pl.loop(0, 20)
+    @pl.loop(0, 32)
     def _(i):
-        pack_block(counts, coeffs, peer_of(i, 1)[1], packed)
+        basis_copy(i).start()
 
     make_tables(slots, gains, me * 4, gram, table, member)
+
+    @pl.loop(0, 8)
+    def _(m):
+        image_copy(m).wait()
+        rows = pl.ds(pl.multiple_of(m * 512, 512), 512)
+        lines = lax.dot_general(
+            forward[...], pixels[rows, :], (((1,), (1,)), ((), ())), preferred_element_type=F32
+        )
+        for n in range(4):
+            spectrum[pl.ds(m * 4 + n, 256, stride=32), :] = lines[:, n * 128 : n * 128 + 128]
+
     pl.semaphore_wait(barrier, 35)
 
     @pl.loop(0, 31)
     def _(i):
         ids_copy(i).start()
 
-    @pl.loop(0, 20)
-    def _(i):
-        data_copy(i).start()
-
-    @pl.loop(20, 32)
-    def _(i):
-        pack_block(counts, coeffs, peer_of(i, 1)[1], packed)
-
-        @pl.when(i < 31)
+    @pl.loop(0, 16)
+    def _(pair):
+        for half in range(2):
+            i = pair * 2 + half
+            basis_copy(i).wait()
+        for half in range(2):
+            pack_block(counts, spectrum, basis, peer_of(pair * 2 + half, 1)[1], packed)
+
+        data_copy(pair * 2).start()
+
+        @pl.when(pair < 15)
         def _():
-            data_copy(i).start()
+            data_copy(pair * 2 + 1).start()
 
     own = pltpu.make_async_copy(packed.at[me], arrived.at[me], local.at[0])
     own.start()
@@ -312,7 +348,7 @@
     parts[quarter] = both
     for copy in copies:
         copy.wait()
-    make_covariances(images, counts, parts, cov_ref, cov_right, size, trace)
+    make_covariances(image_total, counts, parts, cov_ref, cov_right, size, trace)
 
     def send_pair(pair):
         groups = pl.ds(pair * 2, 2)
@@ -344,12 +380,17 @@
                 def _():
                     back_copy(i).start()
 
-    unpack_block(counts, cleaned, me, out)
-
-    @pl.loop(0, 31)
-    def _(i):
-        back_copy(i).wait_recv()
-        unpack_block(counts, returned, peer_of(i, -1)[1], out)
+    unpack_block(counts, cleaned, basis, me, out)
+
+    @pl.loop(0, 15)
+    def _(pair):
+        for half in range(2):
+            back_copy(pair * 2 + half).wait_recv()
+        for half in range(2):
+            unpack_block(counts, returned, basis, peer_of(pair * 2 + half, -1)[1], out)
+
+    back_copy(30).wait_recv()
+    unpack_block(counts, returned, basis, peer_of(30, -1)[1], out)
 
     @pl.loop(0, 31)
     def _(i):
@@ -384,8 +425,12 @@
         excess = (fourth / total - total_of(sample * sample)) / (2.0 * images)
         weight = excess / (excess + spread)
         cov = (1.0 - weight) * sample + (weight * level) * ident
-        cov_ref[j] = cov
-        cov_right[j] = right_side(cov)
+        right = right_side(cov)
+        square = product(cov, right)
+        cov_ref[j, 0] = cov
+        cov_ref[j, 1] = square
+        cov_ref[j, 2] = product(square, right)
+        cov_right[j] = right
         size[j] = jnp.broadcast_to(total_of(cov * cov), (8, 128))
         trace[j] = jnp.broadcast_to(total_of(cov * ident), (8, 128))
 
@@ -404,12 +449,19 @@
         norm = size[j, 0:1, 0:1] * (square * square)
         norm += trace[j, 0:1, 0:1] * (2.0 * square * level) + 128.0 * level * level
         scale = 1.0 / jnp.sqrt(norm)
-        power = (1.0 - scale * level) * ident - (scale * square) * cov_ref[j]
-        powers.append(power)
-        sums.append(ident + power)
+        keep, slope = 1.0 - scale * level, scale * square
+        first, second, third = cov_ref[j, 0], cov_ref[j, 1], cov_ref[j, 2]
+        power = keep * ident - slope * first
+        twice = keep * keep * ident - (2.0 * keep * slope) * first + slope * slope * second
+        thrice = (
+            keep * keep * keep * ident - (3.0 * keep * keep * slope) * first
+            + (3.0 * keep * slope * slope) * second - slope * slope * slope * third
+        )
+        powers.append(twice)
+        sums.append(ident + power + twice + thrice)
         scales.append(scale * gain)
     powers = [product(p, right_side(p)) for p in powers]
-    for _ in range(NS_ITERS - 2):
+    for _ in range(NS_ITERS - 3):
         sides = [right_side(p) for p in powers]
         both = [product(jnp.concatenate([s, p], 0), r) for s, p, r in zip(sums, powers, sides)]
         sums = [s + b[0:128] for s, b in zip(sums, both)]
@@ -451,19 +503,16 @@
 
 
 def dft_tables(angles, freqs):
-    angle_index = jnp.arange(angles, dtype=jnp.int32)
-    freq_index = jnp.arange(freqs, dtype=jnp.int32)
+    angle_index, freq_index = np.arange(angles), np.arange(freqs)
     turns = angle_index[:, None] * freq_index[None, :] % angles
-    phases = turns.astype(jnp.float32) * (2.0 * math.pi / angles)
-    factor = 1.0 / math.sqrt(angles)
-    cosine = jnp.cos(phases) * factor
-    sine = -jnp.sin(phases) * factor
-    forward = jnp.concatenate([cosine, sine], 1).astype(jnp.bfloat16)
-    doubling = jnp.where(freq_index == 0, 1.0, 2.0).astype(jnp.float32)
-    inverse = jnp.concatenate([cosine * doubling[None, :], sine * doubling[None, :]], 1).T.astype(
-        jnp.bfloat16
-    )
-    return (forward, inverse)
+    phases = turns.astype(np.float32) * np.float32(2.0 * math.pi / angles)
+    factor = np.float32(1.0 / math.sqrt(angles))
+    cosine = np.cos(phases) * factor
+    sine = -np.sin(phases) * factor
+    doubling = np.where(freq_index == 0, 1.0, 2.0).astype(np.float32)
+    forward = np.concatenate([cosine, sine], 1).T
+    inverse = np.concatenate([cosine * doubling, sine * doubling], 1).T
+    return forward.astype(BF16), inverse.astype(BF16)
 
 
 def body(images, group_ids, counts, radial_basis, ctf_gain, noise_var):
@@ -472,43 +521,40 @@
     image_total = local_images * lax.axis_size("img") * lax.axis_size("grp")
     dma = pltpu.SemaphoreType.DMA
     forward, inverse = dft_tables(angles, freqs)
-    spectrum = jnp.dot(
-        images.reshape(local_images * radii, angles), forward, preferred_element_type=F32
-    )
-    spectrum = spectrum.astype(BF16).reshape(local_images, radii, 2, freqs)
-    coeffs = jnp.einsum(
-        "nrck,krp->kcnp", spectrum, radial_basis, preferred_element_type=F32
-    ).astype(BF16).reshape(freqs, 64, 128)
     ids = jnp.pad(group_ids, (0, 96)).reshape(1, 128)
     data = pltpu.VMEM((32, 160, 128), BF16)
     sums = pltpu.VMEM((136, 128), F32)
     pairs = pltpu.VMEM((8, 2, 128, 128), BF16)
     small = pltpu.VMEM((2, 8, 128), F32)
-    spread = pl.pallas_call(
+    anywhere = pl.BlockSpec(memory_space=pl.ANY)
+    back = pl.pallas_call(
         functools.partial(main_kernel, image_total),
-        out_shape=jax.ShapeDtypeStruct((freqs, 64, 128), BF16),
-        in_specs=[SMEM, SMEM, SMEM, VMEM, VMEM],
+        out_shape=jax.ShapeDtypeStruct((2 * freqs, local_images, radii), BF16),
+        in_specs=[SMEM, SMEM, SMEM, anywhere, anywhere, VMEM, VMEM],
         out_specs=VMEM,
         scratch_shapes=[
+            pltpu.VMEM((local_images * radii, angles), BF16),
+            pltpu.VMEM((2 * freqs * local_images, radii), F32),
+            pltpu.VMEM(radial_basis.shape, BF16),
             data, data, data, data,
             pltpu.VMEM((32, 1, 128), jnp.int32), pltpu.VMEM((32, 128), F32),
             pltpu.VMEM((3, 512, 128), F32), pltpu.VMEM((128, 512), BF16),
             pltpu.VMEM((384, 128), BF16),
             pltpu.VMEM((2, 136, 128), F32), sums, sums, pltpu.VMEM((4, 136, 128), F32),
-            pltpu.VMEM((2, 128, 128), F32), pltpu.VMEM((2, 256, 256), BF16), small, small,
+            pltpu.VMEM((2, 3, 128, 128), F32), pltpu.VMEM((2, 256, 256), BF16), small, small,
             pairs, pairs, pltpu.VMEM((4, 384, 128), F32), pltpu.VMEM((3072, 384), BF16),
-            dma((2,)), dma((31,)), dma((31,)), dma((31,)), dma((31,)), dma((31,)), dma((31,)),
+            dma((2,)), dma((8,)), dma((32,)),
+            dma((31,)), dma((31,)), dma((31,)), dma((31,)), dma((31,)), dma((31,)),
             dma((8,)), dma((8,)),
         ],
         compiler_params=pltpu.CompilerParams(collective_id=0, has_side_effects=True),
         name="denoise",
-    )(counts, ctf_gain, noise_var, coeffs, ids).reshape(freqs, 2, local_images, 128)
-    back = jnp.einsum(
-        "kcnp,krp->nrck", spread, radial_basis, preferred_element_type=F32
-    ).astype(BF16)
-    back = back.reshape(local_images * radii, 2 * freqs)
-    denoised = jnp.dot(back, inverse, preferred_element_type=F32).astype(BF16)
-    return denoised.reshape(local_images, radii, angles)
+    )(
+        counts, ctf_gain, noise_var, images.reshape(local_images * radii, angles), radial_basis,
+        jnp.asarray(forward), ids,
+    )
+    denoised = jnp.einsum("knr,ka->nra", back, jnp.asarray(inverse), preferred_element_type=F32)
+    return denoised.astype(BF16)
 
 
 def solution(mesh):

time: 103 us -> 88.9 us (0.86)
  matrix products: 15.9 us -> 5.05 us
  local copies, waits for them, and re-layouts: 3.69 us -> 1.17 us
  other arithmetic: 2.24 us -> 0 us
  Pallas kernels: 80.8 us -> 82.3 us
    dot_general x4 -> x1, matrix products: 15.9 us -> 5.05 us  [body(): jnp.einsum('knr,ka->nra', back, jnp.asarray(inverse), preferred_element_t...]
    another operation x2 -> x0, other arithmetic: 2.23 us -> none
    unnamed x3 -> x2, local copies, waits for them, and re-layouts: 2.18 us -> 0.01 us
    pallas_call x1, Pallas kernels: 80.8 us -> 82.3 us  [body(): pl.pallas_call(functools.partial(main_kernel, image_total), out_shape=jax...]
where the time goes in v3:
time: 88.9 us; the launch traced here: 88.5 us
  Pallas kernels  82.3 us (93%)
  matrix products  5.05 us (6%)
  local copies, waits for them, and re-layouts  1.17 us (1%)
    pallas_call x1, Pallas kernels, body(): pl.pallas_call(functools.partial(main_kernel, image_total), out_shape=jax...  82.3 us
    dot_general x1, matrix products, body(): jnp.einsum('knr,ka->nra', back, jnp.asarray(inverse), preferred_element_t...  5.05 us

profile of v3, /device:TPU:1, one launch (start us, length us, event | category | flops | bytes accessed | tf_op | source)
XLA Modules:
  0.0 88.5 jit_solution(1976129165285949889)
XLA Ops:
  0.0 1.2 %pad_bitcast_fusion.my_ids = s32[1,128]{1,0:T(1,128)} fusion(s32[32]{0:T(128)} %param.9), kind=kLoop, calls=%fused_computation.2 | loop fusion | bytes 640 | tf_op jit(solution)/shard_map/reshape | solution.py:524
  1.2 0.0 copy-start
  1.2 82.3 %denoise.1 = bf16[256,32,128]{2,1,0:T(8,128)(2,1)} custom-call(s32[128]{0:T(128)} %counts.1, f32[8,128]{1,0:T(8,128)} %gains.1, f32[128]{0:T(128)} %noise.1, bf16[4096,512]{1,0:T(8,128)(2,1)} %bitcast.5, bf16[128,128,128]{2,1,0:T(8,128)(2,1)} %basis_in.1, bf16[256,512]{1,0:T(8,128)(2,1)} %constant.6.clone.forward, s32[1,128]{1,0:T(1,128)} %pad_bitcast_fusion.my_ids), custom_call_target="tpu_custom_call" | custom-call | tf_op jit(solution)/shard_map/denoise/pallas_call | solution.py:530
  83.5 0.0 copy-done
  83.5 5.1 %convolution_convert_fusion = bf16[32,128,512]{2,1,0:T(8,128)(2,1)} fusion(bf16[256,512,1]{1,0,2:T(8,128)(2,1)S(1)} %copy-done, bf16[256,32,128]{2,1,0:T(8,128)(2,1)} %denoise.1), kind=kOutput, calls=%fused_computation | convolution fusion | flops 1075838976 | bytes 6553600 | tf_op jit(solution)/shard_map/knr,ka->nra/dot_general | solution.py:556
Async XLA Ops:
  1.2 82.3 %copy-start = (bf16[256,512,1]{1,0,2:T(8,128)(2,1)S(1)}, bf16[256,512,1]{1,0,2:T(8,128)(2,1)}, u32[]{:S(2)}) copy-start(bf16[256,512,1]{1,0,2:T(8,128)(2,1)} %constant.12) | copy-start | bytes 786436

commit v4 on v3

--- a/solution.py
+++ b/solution.py
@@ -13,7 +13,6 @@
 SIDE = 4
 MESH_ID = pl.DeviceIdType.MESH
 VMEM = pl.BlockSpec(memory_space=pltpu.VMEM)
-SMEM = pl.BlockSpec(memory_space=pltpu.SMEM)
 F32 = jnp.float32
 BF16 = jnp.bfloat16
 
@@ -126,12 +125,16 @@
     return low, middle, high
 
 
-def chunk_groups(ids, sources):
-    rows = []
-    for s in sources:
-        column = pltpu.roll(ids[...], (128 - s) % 128, 1)[:, 0:1]
-        rows += [jnp.broadcast_to(column, (32, 128))] * 2
-    return jnp.concatenate(rows, 0)
+def store_groups(all_ids, groups, sources):
+    rows = jnp.concatenate([all_ids[s] for s in sources], 0).astype(F32)
+    rows = jnp.concatenate([rows, jnp.zeros((4, 96), F32)], 1)
+    turned = jnp.concatenate([rows, jnp.zeros((124, 128), F32)], 0).T[0:32]
+    for i, s in enumerate(sources):
+        groups[s] = jnp.broadcast_to(turned[:, i : i + 1], (32, 128))
+
+
+def chunk_groups(groups, sources):
+    return jnp.concatenate([r for s in sources for r in [groups[s]] * 2], 0)
 
 
 def make_tables(slots, gains, first_freq, gram, table, member):
@@ -157,12 +160,12 @@
     member[...] = inside.astype(BF16)
 
 
-def add_chunk(packed, ids, sources, gram, table, member, sums):
+def add_chunk(packed, groups, sources, gram, table, member, sums):
     fourth, total = sums
     lane = lanes((256, 128))
     wanted = jnp.where(lane < 24, lane % 8, -1).astype(F32)
     value = jnp.concatenate(chunk_slots(packed, sources), 1)
-    onehot = jnp.where(chunk_groups(ids, sources) == wanted, 1.0, 0.0).astype(BF16)
+    onehot = jnp.where(chunk_groups(groups, sources) == wanted, 1.0, 0.0).astype(BF16)
     gain = jnp.dot(onehot, table[...], preferred_element_type=F32)
     scaled = (value * gain[:, 0:384]).astype(BF16)
     products = lax.dot_general(
@@ -221,27 +224,36 @@
 
 
 def main_kernel(
-    image_total, counts, gains, noise, images, basis_in, forward, my_ids, out,
-    pixels, spectrum, basis, packed, arrived, cleaned, returned, all_ids, ids, gram, table, member,
+    image_total, counts_in, gains_in, noise_in, images, basis_in, forward_in, ids_in, out,
+    counts, gains, noise, forward, my_ids, pixels, spectrum, basis, packed, arrived, cleaned, returned, all_ids, groups, gram, table, member,
     part, other, mine, parts, cov_ref, cov_right, size, trace,
     my_filters, other_filters, shifted, filters,
-    local, load, load_basis, send, recv, send_ids, recv_ids, send_back, recv_back, send_sum, recv_sum,
+    local, load, load_basis, load_small, send, recv, send_ids, recv_ids, send_back, recv_back, send_sum, recv_sum,
 ):
     x, y, z, core = place()
     me = owner_index(x, y, z)
     quarter, low = z // 2, z % 2
-    slots = block_slots(counts, me * 4)
+    smalls = [(counts_in, counts), (gains_in, gains), (noise_in, noise)]
+    smalls += [(forward_in, forward), (ids_in, my_ids)]
+    smalls = [
+        pltpu.make_async_copy(source, target, load_small.at[i])
+        for i, (source, target) in enumerate(smalls)
+    ]
+    for copy in smalls:
+        copy.start()
 
     def image_copy(m):
         rows = pl.ds(pl.multiple_of(m * 512, 512), 512)
         return pltpu.make_async_copy(images.at[rows], pixels.at[rows], load.at[m])
 
-    def basis_copy(i):
-        freqs = pl.ds(peer_of(i, 1)[1] * 4, 4)
-        return pltpu.make_async_copy(basis_in.at[freqs], basis.at[freqs], load_basis.at[i])
+    def basis_copy(m):
+        freqs = pl.ds(m * 32, 32)
+        return pltpu.make_async_copy(basis_in.at[freqs], basis.at[freqs], load_basis.at[m])
 
     for m in range(8):
         image_copy(m).start()
+    for m in range(4):
+        basis_copy(m).start()
     partner = {"img": y * 8 + z, "grp": x * 2 + 1 - core}
     column = []
     for step in (2, 1, 3):
@@ -249,6 +261,9 @@
     barrier = pltpu.get_barrier_semaphore()
     for device in [peer_of(i, 1)[0] for i in range(31)] + [partner] + column:
         pl.semaphore_signal(barrier, inc=1, device_id=device, device_id_type=MESH_ID)
+    for copy in smalls:
+        copy.wait()
+    slots = block_slots(counts, me * 4)
 
     def remote(source, target, sent, received, device):
         return pltpu.make_async_remote_copy(
@@ -268,12 +283,6 @@
 
     def sum_copy(source, target, i, device):
         return remote(source, target, send_sum.at[i], recv_sum.at[i], device)
-
-    @pl.loop(0, 32)
-    def _(i):
-        basis_copy(i).start()
-
-    make_tables(slots, gains, me * 4, gram, table, member)
 
     @pl.loop(0, 8)
     def _(m):
@@ -287,36 +296,30 @@
 
     pl.semaphore_wait(barrier, 35)
 
-    @pl.loop(0, 31)
-    def _(i):
+    for m in range(4):
+        basis_copy(m).wait()
+
+    def send_block(i):
         ids_copy(i).start()
+        data_copy(i).start()
 
     @pl.loop(0, 16)
     def _(pair):
         for half in range(2):
-            i = pair * 2 + half
-            basis_copy(i).wait()
-        for half in range(2):
             pack_block(counts, spectrum, basis, peer_of(pair * 2 + half, 1)[1], packed)
 
-        data_copy(pair * 2).start()
+        send_block(pair * 2)
 
         @pl.when(pair < 15)
         def _():
-            data_copy(pair * 2 + 1).start()
+            send_block(pair * 2 + 1)
 
     own = pltpu.make_async_copy(packed.at[me], arrived.at[me], local.at[0])
     own.start()
     own_ids = pltpu.make_async_copy(my_ids, all_ids.at[me], local.at[1])
     own_ids.start()
+    make_tables(slots, gains, me * 4, gram, table, member)
     own_ids.wait()
-
-    @pl.loop(0, 31)
-    def _(i):
-        ids_copy(i).wait()
-
-    wide = jnp.concatenate([all_ids[s] for s in range(32)], 0).astype(F32)
-    ids[...] = jnp.concatenate([wide, jnp.zeros((96, 128), F32)], 0).T[0:32]
     own.wait()
 
     def chunk(m, sums):
@@ -325,14 +328,17 @@
             i = m * 4 + s
             if s < 3:
                 data_copy(i).wait_recv()
+                ids_copy(i).wait_recv()
             else:
 
                 @pl.when(i < 31)
                 def _():
                     data_copy(i).wait_recv()
+                    ids_copy(i).wait_recv()
 
             sources.append(peer_of(i, -1)[1])
-        return add_chunk(arrived, ids, sources, gram, table, member, sums)
+        store_groups(all_ids, groups, sources)
+        return add_chunk(arrived, groups, sources, gram, table, member, sums)
 
     nothing = jnp.zeros((1, 128), F32)
     gather_grams(slots, gram, lax.fori_loop(0, 8, chunk, (nothing, nothing)), part)
@@ -354,22 +360,27 @@
         groups = pl.ds(pair * 2, 2)
         return sum_copy(my_filters.at[groups], other_filters.at[groups], pair + 4, partner)
 
-    @pl.loop(0, 4)
+    def place_pair(pair):
+        for half in range(2):
+            place_filters(slots, pair * 2 + half, my_filters, other_filters, shifted, filters)
+
+    shifted[...] = jnp.zeros_like(shifted)
+    make_filters(0, gains, noise, my_filters, cov_ref, cov_right, size, trace)
+    send_pair(0).start()
+
+    @pl.loop(1, 4)
     def _(pair):
+        send_pair(pair - 1).wait()
+        place_pair(pair - 1)
         make_filters(pair, gains, noise, my_filters, cov_ref, cov_right, size, trace)
         send_pair(pair).start()
 
-    shifted[...] = jnp.zeros_like(shifted)
-
-    @pl.loop(0, 4)
-    def _(pair):
-        send_pair(pair).wait()
-        for half in range(2):
-            place_filters(slots, pair * 2 + half, my_filters, other_filters, shifted, filters)
+    send_pair(3).wait()
+    place_pair(3)
 
     @pl.loop(0, 8)
     def _(m):
-        apply_chunk(arrived, ids, [peer_of(m * 4 + s, 1)[1] for s in range(4)], filters, cleaned)
+        apply_chunk(arrived, groups, [peer_of(m * 4 + s, 1)[1] for s in range(4)], filters, cleaned)
         for s in range(4):
             i = m * 4 + s
             if s < 3:
@@ -394,6 +405,7 @@
 
     @pl.loop(0, 31)
     def _(i):
+        ids_copy(i).wait_send()
         data_copy(i).wait_send()
         back_copy(i).wait_send()
 
@@ -489,9 +501,9 @@
             filters[row, t * 128 : t * 128 + 128] = tiles[r][t].astype(BF16)
 
 
-def apply_chunk(packed, ids, sources, filters, out):
+def apply_chunk(packed, groups, sources, filters, out):
     value = jnp.concatenate(chunk_slots(packed, sources), 1).astype(BF16)
-    group = chunk_groups(ids, sources)
+    group = chunk_groups(groups, sources)
     pieces = []
     for g in range(8):
         mask = jnp.where(group == float(g), 1.0, 0.0).astype(BF16)
@@ -521,29 +533,32 @@
     image_total = local_images * lax.axis_size("img") * lax.axis_size("grp")
     dma = pltpu.SemaphoreType.DMA
     forward, inverse = dft_tables(angles, freqs)
-    ids = jnp.pad(group_ids, (0, 96)).reshape(1, 128)
+    ids = group_ids.reshape(1, local_images)
     data = pltpu.VMEM((32, 160, 128), BF16)
     sums = pltpu.VMEM((136, 128), F32)
     pairs = pltpu.VMEM((8, 2, 128, 128), BF16)
     small = pltpu.VMEM((2, 8, 128), F32)
-    anywhere = pl.BlockSpec(memory_space=pl.ANY)
+    hbm = pl.BlockSpec(memory_space=pltpu.HBM)
     back = pl.pallas_call(
         functools.partial(main_kernel, image_total),
         out_shape=jax.ShapeDtypeStruct((2 * freqs, local_images, radii), BF16),
-        in_specs=[SMEM, SMEM, SMEM, anywhere, anywhere, VMEM, VMEM],
+        in_specs=[hbm] * 7,
         out_specs=VMEM,
         scratch_shapes=[
+            pltpu.SMEM(counts.shape, jnp.int32), pltpu.SMEM(ctf_gain.shape, F32),
+            pltpu.SMEM(noise_var.shape, F32), pltpu.VMEM(forward.shape, BF16),
+            pltpu.VMEM(ids.shape, jnp.int32),
             pltpu.VMEM((local_images * radii, angles), BF16),
             pltpu.VMEM((2 * freqs * local_images, radii), F32),
             pltpu.VMEM(radial_basis.shape, BF16),
             data, data, data, data,
-            pltpu.VMEM((32, 1, 128), jnp.int32), pltpu.VMEM((32, 128), F32),
+            pltpu.VMEM((32, 1, 32), jnp.int32), pltpu.VMEM((32, 32, 128), F32),
             pltpu.VMEM((3, 512, 128), F32), pltpu.VMEM((128, 512), BF16),
             pltpu.VMEM((384, 128), BF16),
             pltpu.VMEM((2, 136, 128), F32), sums, sums, pltpu.VMEM((4, 136, 128), F32),
             pltpu.VMEM((2, 3, 128, 128), F32), pltpu.VMEM((2, 256, 256), BF16), small, small,
             pairs, pairs, pltpu.VMEM((4, 384, 128), F32), pltpu.VMEM((3072, 384), BF16),
-            dma((2,)), dma((8,)), dma((32,)),
+            dma((2,)), dma((8,)), dma((4,)), dma((5,)),
             dma((31,)), dma((31,)), dma((31,)), dma((31,)), dma((31,)), dma((31,)),
             dma((8,)), dma((8,)),
         ],

time: 88.9 us -> 90.9 us (1.022)
  Pallas kernels: 82.3 us -> 85.7 us
  local copies, waits for them, and re-layouts: 1.17 us -> 0.01 us
    pallas_call x1, Pallas kernels: 82.3 us -> 85.7 us  [body(): pl.pallas_call(functools.partial(main_kernel, image_total), out_shape=jax...]
    reshape x1 -> x0, local copies, waits for them, and re-layouts: 1.17 us -> none  [body(): ids = jnp.pad(group_ids, (0, 96)).reshape(1, 128)]
where the time goes in v4:
time: 90.9 us; the launch traced here: 90.8 us
  Pallas kernels  85.7 us (94%)
  matrix products  5.05 us (6%)
    pallas_call x1, Pallas kernels, body(): pl.pallas_call(functools.partial(main_kernel, image_total), out_shape=jax...  85.7 us
    dot_general x1, matrix products, body(): jnp.einsum('knr,ka->nra', back, jnp.asarray(inverse), preferred_element_t...  5.05 us

profile of v4, /device:TPU:1, one launch (start us, length us, event | category | flops | bytes accessed | tf_op | source)
XLA Modules:
  0.0 90.8 jit_solution(793795489259212697)
XLA Ops:
  0.0 0.0 copy-start
  0.0 85.7 %denoise.1 = bf16[256,32,128]{2,1,0:T(8,128)(2,1)} custom-call(s32[128]{0:T(128)} %counts_in.1, f32[8,128]{1,0:T(8,128)} %gains_in.1, f32[128]{0:T(128)} %noise_in.1, bf16[4096,512]{1,0:T(8,128)(2,1)} %bitcast.4, bf16[128,128,128]{2,1,0:T(8,128)(2,1)} %basis_in.1, bf16[256,512]{1,0:T(8,128)(2,1)} %constant.4.clone.forward_in, s32[1,32]{1,0:T(1,128)} %bitcast.5), custom_call_target="tpu_custom_call" | custom-call | tf_op jit(solution)/shard_map/denoise/pallas_call | solution.py:542
  85.7 0.0 copy-done
  85.7 5.1 %convolution_convert_fusion = bf16[32,128,512]{2,1,0:T(8,128)(2,1)} fusion(bf16[256,512,1]{1,0,2:T(8,128)(2,1)S(1)} %copy-done, bf16[256,32,128]{2,1,0:T(8,128)(2,1)} %denoise.1), kind=kOutput, calls=%fused_computation | convolution fusion | flops 1075838976 | bytes 6553600 | tf_op jit(solution)/shard_map/knr,ka->nra/dot_general | solution.py:571
Async XLA Ops:
  0.0 85.7 %copy-start = (bf16[256,512,1]{1,0,2:T(8,128)(2,1)S(1)}, bf16[256,512,1]{1,0,2:T(8,128)(2,1)}, u32[]{:S(2)}) copy-start(bf16[256,512,1]{1,0,2:T(8,128)(2,1)} %constant.8) | copy-start | bytes 786436

commit v5 on v4

--- a/solution.py
+++ b/solution.py
@@ -17,26 +17,34 @@
 BF16 = jnp.bfloat16
 
 
+def rem(a, n):
+    return a % n if isinstance(a, int) else lax.rem(a, jnp.int32(n))
+
+
+def div(a, n):
+    return a // n if isinstance(a, int) else lax.div(a, jnp.int32(n))
+
+
 def place():
     img = lax.axis_index("img")
     grp = lax.axis_index("grp")
-    return grp // 2, img // 8, img % 8, grp % 2
+    return div(grp, 2), div(img, 8), rem(img, 8), rem(grp, 2)
 
 
 def owner_index(x, y, z):
-    return x * 8 + y * 2 + z % 2
+    return x * 8 + y * 2 + rem(z, 2)
 
 
 def step_of(i):
-    turn = i % 4
-    return (turn + 1) % 4, (i // 4 + turn + 2) % 4, 1 - i // 16
+    turn = rem(i, 4)
+    return rem(turn + 1, 4), rem(div(i, 4) + turn + 2, 4), 1 - div(i, 16)
 
 
 def peer_of(i, sign):
     x, y, z, core = place()
     a, b, c = step_of(i)
-    px, py = (x + SIDE + sign * a) % SIDE, (y + SIDE + sign * b) % SIDE
-    pz = z // 2 * 2 + (z + c) % 2
+    px, py = rem(x + SIDE + sign * a, SIDE), rem(y + SIDE + sign * b, SIDE)
+    pz = div(z, 2) * 2 + rem(z + c, 2)
     return {"img": py * 8 + pz, "grp": px * 2 + core}, owner_index(px, py, pz)
 
 
@@ -352,6 +360,13 @@
     for copy in copies:
         copy.start()
     parts[quarter] = both
+    shifted[...] = jnp.zeros_like(shifted)
+
+    @pl.loop(0, 31)
+    def _(i):
+        ids_copy(i).wait_send()
+        data_copy(i).wait_send()
+
     for copy in copies:
         copy.wait()
     make_covariances(image_total, counts, parts, cov_ref, cov_right, size, trace)
@@ -364,19 +379,15 @@
         for half in range(2):
             place_filters(slots, pair * 2 + half, my_filters, other_filters, shifted, filters)
 
-    shifted[...] = jnp.zeros_like(shifted)
-    make_filters(0, gains, noise, my_filters, cov_ref, cov_right, size, trace)
-    send_pair(0).start()
-
-    @pl.loop(1, 4)
+    @pl.loop(0, 4)
     def _(pair):
-        send_pair(pair - 1).wait()
-        place_pair(pair - 1)
         make_filters(pair, gains, noise, my_filters, cov_ref, cov_right, size, trace)
         send_pair(pair).start()
 
-    send_pair(3).wait()
-    place_pair(3)
+    @pl.loop(0, 4)
+    def _(pair):
+        send_pair(pair).wait()
+        place_pair(pair)
 
     @pl.loop(0, 8)
     def _(m):
@@ -396,18 +407,12 @@
     @pl.loop(0, 15)
     def _(pair):
         for half in range(2):
-            back_copy(pair * 2 + half).wait_recv()
+            back_copy(pair * 2 + half).wait()
         for half in range(2):
             unpack_block(counts, returned, basis, peer_of(pair * 2 + half, -1)[1], out)
 
-    back_copy(30).wait_recv()
+    back_copy(30).wait()
     unpack_block(counts, returned, basis, peer_of(30, -1)[1], out)
-
-    @pl.loop(0, 31)
-    def _(i):
-        ids_copy(i).wait_send()
-        data_copy(i).wait_send()
-        back_copy(i).wait_send()
 
 
 def make_covariances(images, counts, parts, cov_ref, cov_right, size, trace):

time: 90.9 us -> 85.8 us (0.944)
  Pallas kernels: 85.7 us -> 80.6 us
    pallas_call x1, Pallas kernels: 85.7 us -> 80.6 us  [body(): pl.pallas_call(functools.partial(main_kernel, image_total), out_shape=jax...]
where the time goes in v5:
time: 85.8 us; the launch traced here: 85.7 us
  Pallas kernels  80.6 us (94%)
  matrix products  5.06 us (6%)
    pallas_call x1, Pallas kernels, body(): pl.pallas_call(functools.partial(main_kernel, image_total), out_shape=jax...  80.6 us
    dot_general x1, matrix products, body(): jnp.einsum('knr,ka->nra', back, jnp.asarray(inverse), preferred_element_t...  5.06 us

profile of v5, /device:TPU:1, one launch (start us, length us, event | category | flops | bytes accessed | tf_op | source)
XLA Modules:
  0.0 85.7 jit_solution(5849249112279236696)
XLA Ops:
  0.0 0.0 copy-start
  0.0 80.6 %denoise.1 = bf16[256,32,128]{2,1,0:T(8,128)(2,1)} custom-call(s32[128]{0:T(128)} %counts_in.1, f32[8,128]{1,0:T(8,128)} %gains_in.1, f32[128]{0:T(128)} %noise_in.1, bf16[4096,512]{1,0:T(8,128)(2,1)} %bitcast.4, bf16[128,128,128]{2,1,0:T(8,128)(2,1)} %basis_in.1, bf16[256,512]{1,0:T(8,128)(2,1)} %constant.4.clone.forward_in, s32[1,32]{1,0:T(1,128)} %bitcast.5), custom_call_target="tpu_custom_call" | custom-call | tf_op jit(solution)/shard_map/denoise/pallas_call | solution.py:547
  80.6 0.0 copy-done
  80.6 5.1 %convolution_convert_fusion = bf16[32,128,512]{2,1,0:T(8,128)(2,1)} fusion(bf16[256,512,1]{1,0,2:T(8,128)(2,1)S(1)} %copy-done, bf16[256,32,128]{2,1,0:T(8,128)(2,1)} %denoise.1), kind=kOutput, calls=%fused_computation | convolution fusion | flops 1075838976 | bytes 6553600 | tf_op jit(solution)/shard_map/knr,ka->nra/dot_general | solution.py:576
Async XLA Ops:
  0.0 80.6 %copy-start = (bf16[256,512,1]{1,0,2:T(8,128)(2,1)S(1)}, bf16[256,512,1]{1,0,2:T(8,128)(2,1)}, u32[]{:S(2)}) copy-start(bf16[256,512,1]{1,0,2:T(8,128)(2,1)} %constant.8) | copy-start | bytes 786436

commit v6 on v5

--- a/solution.py
+++ b/solution.py
@@ -12,7 +12,6 @@
 NS_ITERS = 7
 SIDE = 4
 MESH_ID = pl.DeviceIdType.MESH
-VMEM = pl.BlockSpec(memory_space=pltpu.VMEM)
 F32 = jnp.float32
 BF16 = jnp.bfloat16
 
@@ -108,7 +107,7 @@
     return pltpu.roll(picked, (128 - offset % 128) % 128, 1)
 
 
-def unpack_block(counts, packed, basis, block, out):
+def unpack_block(counts, packed, basis, block, out, out_hbm, sent):
     lane = lanes((64, 128))
     tiles = [
         packed[block, 0:64].astype(F32),
@@ -123,6 +122,9 @@
         ).astype(BF16)
         for c in range(2):
             out[c * 128 + freq] = back[c * 32 : c * 32 + 32]
+    for c in range(2):
+        rows = pl.ds(c * 128 + block * 4, 4)
+        pltpu.make_async_copy(out.at[rows], out_hbm.at[rows], sent).start()
 
 
 def chunk_slots(packed, sources):
@@ -232,10 +234,10 @@
 
 
 def main_kernel(
-    image_total, counts_in, gains_in, noise_in, images, basis_in, forward_in, ids_in, out,
-    counts, gains, noise, forward, my_ids, pixels, spectrum, basis, packed, arrived, cleaned, returned, all_ids, groups, gram, table, member,
+    image_total, counts_in, gains_in, noise_in, images, basis_in, forward_in, ids_in, out_hbm,
+    out, counts, gains, noise, forward, my_ids, pixels, spectrum, basis, packed, arrived, cleaned, returned, all_ids, groups, gram, table, member,
     part, other, mine, parts, cov_ref, cov_right, size, trace,
-    my_filters, other_filters, shifted, filters,
+    my_filters, other_filters, shifted, filters, filters_last,
     local, load, load_basis, load_small, send, recv, send_ids, recv_ids, send_back, recv_back, send_sum, recv_sum,
 ):
     x, y, z, core = place()
@@ -251,14 +253,14 @@
         copy.start()
 
     def image_copy(m):
-        rows = pl.ds(pl.multiple_of(m * 512, 512), 512)
+        rows = pl.ds(pl.multiple_of(m * 1024, 1024), 1024)
         return pltpu.make_async_copy(images.at[rows], pixels.at[rows], load.at[m])
 
     def basis_copy(m):
         freqs = pl.ds(m * 32, 32)
         return pltpu.make_async_copy(basis_in.at[freqs], basis.at[freqs], load_basis.at[m])
 
-    for m in range(8):
+    for m in range(4):
         image_copy(m).start()
     for m in range(4):
         basis_copy(m).start()
@@ -292,15 +294,15 @@
     def sum_copy(source, target, i, device):
         return remote(source, target, send_sum.at[i], recv_sum.at[i], device)
 
-    @pl.loop(0, 8)
+    @pl.loop(0, 4)
     def _(m):
         image_copy(m).wait()
-        rows = pl.ds(pl.multiple_of(m * 512, 512), 512)
+        rows = pl.ds(pl.multiple_of(m * 1024, 1024), 1024)
         lines = lax.dot_general(
             forward[...], pixels[rows, :], (((1,), (1,)), ((), ())), preferred_element_type=F32
         )
-        for n in range(4):
-            spectrum[pl.ds(m * 4 + n, 256, stride=32), :] = lines[:, n * 128 : n * 128 + 128]
+        for n in range(8):
+            spectrum[pl.ds(m * 8 + n, 256, stride=32), :] = lines[:, n * 128 : n * 128 + 128]
 
     pl.semaphore_wait(barrier, 35)
 
@@ -377,12 +379,15 @@
 
     def place_pair(pair):
         for half in range(2):
-            place_filters(slots, pair * 2 + half, my_filters, other_filters, shifted, filters)
-
-    @pl.loop(0, 4)
-    def _(pair):
-        make_filters(pair, gains, noise, my_filters, cov_ref, cov_right, size, trace)
-        send_pair(pair).start()
+            place_filters(
+                slots, pair, half, my_filters, other_filters, shifted, filters, filters_last
+            )
+
+    @pl.loop(0, 2)
+    def _(half):
+        make_filters(half, gains, noise, my_filters, cov_ref, cov_right, size, trace)
+        for pair in range(2):
+            send_pair(half * 2 + pair).start()
 
     @pl.loop(0, 4)
     def _(pair):
@@ -391,7 +396,8 @@
 
     @pl.loop(0, 8)
     def _(m):
-        apply_chunk(arrived, groups, [peer_of(m * 4 + s, 1)[1] for s in range(4)], filters, cleaned)
+        sources = [peer_of(m * 4 + s, 1)[1] for s in range(4)]
+        apply_chunk(arrived, groups, sources, filters, filters_last, cleaned)
         for s in range(4):
             i = m * 4 + s
             if s < 3:
@@ -402,17 +408,19 @@
                 def _():
                     back_copy(i).start()
 
-    unpack_block(counts, cleaned, basis, me, out)
+    unpack_block(counts, cleaned, basis, me, out, out_hbm, local.at[2])
 
     @pl.loop(0, 15)
     def _(pair):
         for half in range(2):
             back_copy(pair * 2 + half).wait()
         for half in range(2):
-            unpack_block(counts, returned, basis, peer_of(pair * 2 + half, -1)[1], out)
+            index = peer_of(pair * 2 + half, -1)[1]
+            unpack_block(counts, returned, basis, index, out, out_hbm, local.at[2])
 
     back_copy(30).wait()
-    unpack_block(counts, returned, basis, peer_of(30, -1)[1], out)
+    unpack_block(counts, returned, basis, peer_of(30, -1)[1], out, out_hbm, local.at[2])
+    pltpu.make_async_copy(out, out_hbm, local.at[2]).wait()
 
 
 def make_covariances(images, counts, parts, cov_ref, cov_right, size, trace):
@@ -458,7 +466,7 @@
     ident = jnp.where(
         lax.broadcasted_iota(jnp.int32, (128, 128), 0) == lanes((128, 128)), 1.0, 0.0
     )
-    problems = [(pair * 2 + g, j) for g in range(2) for j in range(2)]
+    problems = [(pair * 4 + g, j) for g in range(4) for j in range(2)]
     powers, sums, scales = [], [], []
     for g, j in problems:
         gain, level = gains[g, first_freq + j], noise[first_freq + j]
@@ -488,7 +496,8 @@
         out[g, j] = (scale * product(s, cov_right[j])).astype(BF16)
 
 
-def place_filters(slots, g, mine, other, shifted, filters):
+def place_filters(slots, pair, half, mine, other, shifted, filters, filters_last):
+    g = pair * 2 + half
     core = place()[3]
     lane = lanes((128, 128))
     tiles = [[jnp.zeros((128, 128), F32)] * 3 for _ in range(3)]
@@ -498,22 +507,44 @@
         for r in range(3):
             start = jnp.clip(r * 128 + 128 - offset, 0, 256)
             rows = shifted[j, pl.ds(start, 128)]
-            for t in range(3):
-                tiles[r][t] += jnp.where(slot_mask(lane, t, offset, count), rows, 0.0)
-    for r in range(3):
-        row = pl.ds(pl.multiple_of(g * 384 + r * 128, 128), 128)
-        for t in range(3):
-            filters[row, t * 128 : t * 128 + 128] = tiles[r][t].astype(BF16)
-
-
-def apply_chunk(packed, groups, sources, filters, out):
-    value = jnp.concatenate(chunk_slots(packed, sources), 1).astype(BF16)
+            for t in range(max(r - 1, 0), min(r + 2, 3)):
+                tiles[r][t] = jnp.where(slot_mask(lane, t, offset, count), rows, tiles[r][t])
+    for t in range(2):
+        column = slice(t * 128, t * 128 + 128)
+        for r in range(2):
+            row = pl.ds(pl.multiple_of(g * 256 + r * 128, 128), 128)
+            filters[row, column] = tiles[r][t].astype(BF16)
+        filters[pl.ds(pl.multiple_of(2048 + pair * 128 + half * 64, 64), 64), column] = (
+            tiles[2][t][0:64].astype(BF16)
+        )
+    filters_last[pl.ds(pl.multiple_of(g * 128, 128), 128), :] = tiles[1][2].astype(BF16)
+    filters_last[pl.ds(pl.multiple_of(1024 + pair * 128 + half * 64, 64), 64), :] = (
+        tiles[2][2][0:64].astype(BF16)
+    )
+
+
+def apply_chunk(packed, groups, sources, filters, filters_last, out):
+    low, middle, high = chunk_slots(packed, sources)
+    both = jnp.concatenate([low, middle], 1).astype(BF16)
+    twice = (high + pltpu.roll(high, 64, 1)).astype(BF16)
     group = chunk_groups(groups, sources)
-    pieces = []
+    second = jnp.where(lanes((256, 128)) >= 64, 1.0, 0.0)
+    pieces, ends = [], []
     for g in range(8):
         mask = jnp.where(group == float(g), 1.0, 0.0).astype(BF16)
-        pieces.append(value * jnp.concatenate([mask] * 3, 1))
-    cleaned = jnp.dot(jnp.concatenate(pieces, 1), filters[...], preferred_element_type=F32)
+        pieces.append(both * jnp.concatenate([mask] * 2, 1))
+    for pair in range(4):
+        mask = jnp.where(group - second == float(pair * 2), 1.0, 0.0).astype(BF16)
+        ends.append(twice * mask)
+    left = jnp.concatenate(pieces + ends, 1)
+    right = jnp.concatenate([p[:, 128:256] for p in pieces] + ends, 1)
+    cleaned = jnp.concatenate(
+        [
+            jnp.dot(left, filters[...], preferred_element_type=F32),
+            jnp.dot(right, filters_last[...], preferred_element_type=F32),
+        ],
+        1,
+    )
     for s, source in enumerate(sources):
         rows = cleaned[s * 64 : s * 64 + 64]
         fold_slots(rows[:, 0:128], rows[:, 128:256], rows[:, 256:384], out.at[source])
@@ -548,8 +579,9 @@
         functools.partial(main_kernel, image_total),
         out_shape=jax.ShapeDtypeStruct((2 * freqs, local_images, radii), BF16),
         in_specs=[hbm] * 7,
-        out_specs=VMEM,
+        out_specs=hbm,
         scratch_shapes=[
+            pltpu.VMEM((2 * freqs, local_images, radii), BF16),
             pltpu.SMEM(counts.shape, jnp.int32), pltpu.SMEM(ctf_gain.shape, F32),
             pltpu.SMEM(noise_var.shape, F32), pltpu.VMEM(forward.shape, BF16),
             pltpu.VMEM(ids.shape, jnp.int32),
@@ -562,8 +594,9 @@
             pltpu.VMEM((384, 128), BF16),
             pltpu.VMEM((2, 136, 128), F32), sums, sums, pltpu.VMEM((4, 136, 128), F32),
             pltpu.VMEM((2, 3, 128, 128), F32), pltpu.VMEM((2, 256, 256), BF16), small, small,
-            pairs, pairs, pltpu.VMEM((4, 384, 128), F32), pltpu.VMEM((3072, 384), BF16),
-            dma((2,)), dma((8,)), dma((4,)), dma((5,)),
+            pairs, pairs, pltpu.VMEM((4, 384, 128), F32), pltpu.VMEM((2560, 256), BF16),
+            pltpu.VMEM((1536, 128), BF16),
+            dma((3,)), dma((4,)), dma((4,)), dma((5,)),
             dma((31,)), dma((31,)), dma((31,)), dma((31,)), dma((31,)), dma((31,)),
             dma((8,)), dma((8,)),
         ],

time: 85.8 us -> 81.3 us (0.948)
  Pallas kernels: 80.6 us -> 76.2 us
    pallas_call x1, Pallas kernels: 80.6 us -> 76.2 us  [body(): pl.pallas_call(functools.partial(main_kernel, image_total), out_shape=jax...]
where the time goes in v6:
time: 81.3 us; the launch traced here: 81.2 us
  Pallas kernels  76.2 us (94%)
  matrix products  5.05 us (6%)
    pallas_call x1, Pallas kernels, body(): pl.pallas_call(functools.partial(main_kernel, image_total), out_shape=jax...  76.2 us
    dot_general x1, matrix products, body(): jnp.einsum('knr,ka->nra', back, jnp.asarray(inverse), preferred_element_t...  5.05 us

profile of v6, /device:TPU:1, one launch (start us, length us, event | category | flops | bytes accessed | tf_op | source)
XLA Modules:
  0.0 81.2 jit_solution(8493569297466959871)
XLA Ops:
  0.0 0.0 copy-start
  0.0 76.2 %denoise.1 = bf16[256,32,128]{2,1,0:T(8,128)(2,1)} custom-call(s32[128]{0:T(128)} %counts_in.1, f32[8,128]{1,0:T(8,128)} %gains_in.1, f32[128]{0:T(128)} %noise_in.1, bf16[4096,512]{1,0:T(8,128)(2,1)} %bitcast.4, bf16[128,128,128]{2,1,0:T(8,128)(2,1)} %basis_in.1, bf16[256,512]{1,0:T(8,128)(2,1)} %constant.4.clone.forward_in, s32[1,32]{1,0:T(1,128)} %bitcast.5), custom_call_target="tpu_custom_call" | custom-call | tf_op jit(solution)/shard_map/denoise/pallas_call | solution.py:578
  76.2 0.0 copy-done
  76.2 5.1 %convolution_convert_fusion = bf16[32,128,512]{2,1,0:T(8,128)(2,1)} fusion(bf16[256,512,1]{1,0,2:T(8,128)(2,1)S(1)} %copy-done, bf16[256,32,128]{2,1,0:T(8,128)(2,1)} %denoise.1), kind=kOutput, calls=%fused_computation | convolution fusion | flops 1075838976 | bytes 6553600 | tf_op jit(solution)/shard_map/knr,ka->nra/dot_general | solution.py:609
Async XLA Ops:
  0.0 76.2 %copy-start = (bf16[256,512,1]{1,0,2:T(8,128)(2,1)S(1)}, bf16[256,512,1]{1,0,2:T(8,128)(2,1)}, u32[]{:S(2)}) copy-start(bf16[256,512,1]{1,0,2:T(8,128)(2,1)} %constant.8) | copy-start | bytes 786436

commit v7 on v6

--- a/solution.py
+++ b/solution.py
@@ -36,7 +36,7 @@
 
 def step_of(i):
     turn = rem(i, 4)
-    return rem(turn + 1, 4), rem(div(i, 4) + turn + 2, 4), 1 - div(i, 16)
+    return rem(turn + 1, 4), rem(div(i, 4) + turn + 2, 4), rem(turn + div(i, 4) + div(i, 16) + 1, 2)
 
 
 def peer_of(i, sign):

time: 81.3 us -> 77.3 us (0.951)
  Pallas kernels: 76.2 us -> 72.1 us
    pallas_call x1, Pallas kernels: 76.2 us -> 72.1 us  [body(): pl.pallas_call(functools.partial(main_kernel, image_total), out_shape=jax...]
where the time goes in v7:
time: 77.3 us; the launch traced here: 77.2 us
  Pallas kernels  72.1 us (93%)
  matrix products  5.05 us (7%)
    pallas_call x1, Pallas kernels, body(): pl.pallas_call(functools.partial(main_kernel, image_total), out_shape=jax...  72.1 us
    dot_general x1, matrix products, body(): jnp.einsum('knr,ka->nra', back, jnp.asarray(inverse), preferred_element_t...  5.05 us

profile of v7, /device:TPU:1, one launch (start us, length us, event | category | flops | bytes accessed | tf_op | source)
XLA Modules:
  0.0 77.2 jit_solution(9326560388576844323)
XLA Ops:
  0.0 0.0 copy-start
  0.0 72.1 %denoise.1 = bf16[256,32,128]{2,1,0:T(8,128)(2,1)} custom-call(s32[128]{0:T(128)} %counts_in.1, f32[8,128]{1,0:T(8,128)} %gains_in.1, f32[128]{0:T(128)} %noise_in.1, bf16[4096,512]{1,0:T(8,128)(2,1)} %bitcast.4, bf16[128,128,128]{2,1,0:T(8,128)(2,1)} %basis_in.1, bf16[256,512]{1,0:T(8,128)(2,1)} %constant.4.clone.forward_in, s32[1,32]{1,0:T(1,128)} %bitcast.5), custom_call_target="tpu_custom_call" | custom-call | tf_op jit(solution)/shard_map/denoise/pallas_call | solution.py:578
  72.1 0.0 copy-done
  72.1 5.1 %convolution_convert_fusion = bf16[32,128,512]{2,1,0:T(8,128)(2,1)} fusion(bf16[256,512,1]{1,0,2:T(8,128)(2,1)S(1)} %copy-done, bf16[256,32,128]{2,1,0:T(8,128)(2,1)} %denoise.1), kind=kOutput, calls=%fused_computation | convolution fusion | flops 1075838976 | bytes 6553600 | tf_op jit(solution)/shard_map/knr,ka->nra/dot_general | solution.py:609
Async XLA Ops:
  0.0 72.1 %copy-start = (bf16[256,512,1]{1,0,2:T(8,128)(2,1)S(1)}, bf16[256,512,1]{1,0,2:T(8,128)(2,1)}, u32[]{:S(2)}) copy-start(bf16[256,512,1]{1,0,2:T(8,128)(2,1)} %constant.8) | copy-start | bytes 786436
